TPU v7x, 32 devices: a whole 2x2x4 slice. The times are simulated.
32 devices in a mesh: gx: 2 (over x), gy: 4 (over z), gz: 4 (over y, core).
Axes of the slice: x: 2, y: 2, z: 4, core: 2. Of those that a mesh axis runs over, the one named last changes fastest.
Arguments:
- fields: float32 [12, 16, 32, 512], P(None, 'gx', 'gy', 'gz'), as said below
- reacting: int32 [16, 32, 512], P('gx', 'gy', 'gz'), may hold values from 0 to 1, as said below
- panel_map: int32 [2, 16, 512], P(None, 'gx', 'gz'), may hold values from 0 to 255, as said below
- layer_one: bfloat16 [1600, 12], replicated, may hold values from -4 to 4
- layer_two: bfloat16 [800, 1600], replicated, may hold values from -0.21875 to 0.21875
- layer_three: bfloat16 [400, 800], replicated, may hold values from -0.3125 to 0.3125
- layer_four: bfloat16 [12, 400], replicated, may hold values from -0.3125 to 0.3125
Outputs:
- new_fields: float32 [12, 16, 32, 512], P(None, 'gx', 'gy', 'gz')
- impulse: float32 [256], P(('gx', 'gy', 'gz'))
Inputs may be any that keep to these rules, and one draw needn't show every extreme that they name: `fields`: component 0 (density) lies between 0.3 and 3.3; the velocities (components 1 to 3 over component 0) between -1.2 and 1.2; the pressure 0.4 (component 4 - |momentum|^2 / (2 density)) between 0.3 and 5; components 5 to 11 are 0.01 to 0.14 times component 0. Each device's aligned block of 8 x 8 x 128 cells holds at most 128 reacting cells. The blocks that share their ranges along the second and third dimensions hold exactly 64 reacting cells each on average, and one in eight of them, and at least one, hold exactly 128. `panel_map`: every panel is a patch of 8 x 8 cells of one wall, shifted by 4 cells along the first dimension and closed around it; panels are numbered in a random order and each number is used once.
All inputs are finite; a program needn't handle non-finite values.
Results may differ from a plain program's by a relative error of at most 0.0014.
Values may be sent and summed in bfloat16 or wider, within the bound.
No kernel may reach another device: no remote copies, remote signals or barrier semaphores. Data moves between devices by JAX's collectives and lax.ppermute only.
A program may use at most 64 MiB of HBM per device.

v0:
```python
import jax
import jax.numpy as jnp
from jax import lax
from jax.experimental import pallas as pl
from jax.experimental.pallas import tpu as pltpu
from jax.sharding import PartitionSpec as P


BAL = 64
COMPS = 12
PATCH = 8

HEAT_RATIO = 1.4
TIME_STEP = 0.1
CHEM_STEP = 0.25
WENO_EPS = 1e-06
EPS = WENO_EPS * 4.0 / 36.0
AXES = ("gx", "gy", "gz")
F32 = jnp.float32
BF16 = jnp.bfloat16
GRANT = pltpu.CompilerParams(vmem_limit_bytes=12 * 2**20)
VM = pl.BlockSpec(memory_space=pltpu.VMEM)
HBM = pl.BlockSpec(memory_space=pltpu.HBM)


def weno_line(v):
    n = len(v)
    d = [(v[j + 1] - v[j]) * (1.0 / 6.0) for j in range(n - 1)]
    d3 = [3.0 * x for x in d]
    q = {}
    for e in range(1, n - 1):
        s = d[e] - d[e - 1]
        q[e] = (13.0 / 3.0) * (s * s) + EPS
    upper, lower = {}, {}
    for e in range(2, n - 2):
        dm, dp = d[e - 1], d[e]
        t0 = d3[e - 1] - d[e - 2]
        t1 = dm + dp
        t2 = d3[e] - d[e + 1]
        b0 = q[e - 1] + t0 * t0
        b1 = q[e] + t1 * t1
        b2 = q[e + 1] + t2 * t2
        m01, m02, m12 = b0 * b1, b0 * b2, b1 * b2
        s01, s02, s12 = m01 * m01, m02 * m02, m12 * m12
        w1, w01, w12 = 6.0 * s02, 3.0 * s01, 3.0 * s12
        if e < n - 3:
            num = s12 * (t0 + t0 - dm) + w1 * (t1 + dp) + w01 * (t2 + dp)
            upper[e] = v[e] + num / (s12 + w1 + w01)
        if e > 2:
            num = s01 * (t2 + t2 - dp) + w1 * (t1 + dm) + w12 * (t0 + dm)
            lower[e] = v[e] - num / (s01 + w1 + w12)
    return upper, lower


def weno_one(v):
    d = [(v[j + 1] - v[j]) * (1.0 / 6.0) for j in range(4)]
    s = [d[j + 1] - d[j] for j in range(3)]
    q = [(13.0 / 3.0) * (x * x) + EPS for x in s]
    dm, dp = d[1], d[2]
    t0, t1, t2 = 3.0 * dm - d[0], dm + dp, 3.0 * dp - d[3]
    b0, b1, b2 = q[0] + t0 * t0, q[1] + t1 * t1, q[2] + t2 * t2
    m01, m02, m12 = b0 * b1, b0 * b2, b1 * b2
    w0, w1, w2 = m12 * m12, 6.0 * (m02 * m02), 3.0 * (m01 * m01)
    num = w0 * (t0 + t0 - dm) + w1 * (t1 + dp) + w2 * (t2 + dp)
    return v[2] + num / (w0 + w1 + w2)


def hllc(left, right, normal):
    n = 1 + normal

    def side(x):
        rho = jnp.exp(x[0])
        g = jnp.exp(0.5 * (x[4] - x[0]))
        h = g * g
        return rho, h, rho * h, (HEAT_RATIO**0.5) * g, x[n]

    rho_l, h_l, p_l, c_l, u_l = side(left)
    rho_r, h_r, p_r, c_r, u_r = side(right)
    s_l = jnp.minimum(u_l - c_l, u_r - c_r)
    s_r = jnp.maximum(u_l + c_l, u_r + c_r)
    m_l = rho_l * (s_l - u_l)
    m_r = rho_r * (s_r - u_r)
    s = (p_r - p_l + u_l * m_l - u_r * m_r) / (m_l - m_r)
    use_l = (s >= 0) | (s_l >= 0)
    pick = [jnp.where(use_l, a, b) for a, b in zip(left, right)]
    rho = jnp.where(use_l, rho_l, rho_r)
    h = jnp.where(use_l, h_l, h_r)
    p = jnp.where(use_l, p_l, p_r)
    wave = jnp.where(use_l, s_l, s_r)
    act = jnp.where(use_l, jnp.minimum(s_l, 0.0), jnp.maximum(s_r, 0.0))
    u = pick[n]
    rel = s - u
    ratio = rel / (wave - s)
    mass = rho * (u + act * ratio)
    k = rho * act * (1.0 + ratio) * rel
    square = pick[1] * pick[1] + pick[2] * pick[2] + pick[3] * pick[3]
    enthalpy = (1.0 / (HEAT_RATIO - 1.0) + 1.0) * h + 0.5 * square
    flux = [mass * x for x in pick]
    flux[0] = mass
    flux[n] = flux[n] + (p + k)
    flux[4] = enthalpy * mass + k * s
    return flux


def place_flags():
    sizes = [lax.axis_size(a) for a in AXES]
    index = [lax.axis_index(a) for a in AXES]
    place = (index[0] * sizes[1] + index[1]) * sizes[2] + index[2]
    flags = [f for i, n in zip(index, sizes) for f in (i == 0, i == n - 1)]
    return flags + [lax.rem(i, 2) for i in index] + [place]


def rows8(index):
    return pl.ds(pl.multiple_of(index * 8, 8), 8)


def face_states(load_line, left_ref, right_ref, faces):
    def one(c, carry):
        upper, lower = weno_line(load_line(c))
        for f in range(faces):
            left_ref[rows8(c * faces + f), :] = upper[f + 2]
            right_ref[rows8(c * faces + f), :] = lower[f + 3]
        return carry

    lax.fori_loop(0, COMPS, one, 0)


def line_changes(left_ref, right_ref, faces, normal, emit):
    before = None
    for f in range(faces):
        left = [left_ref[pl.ds((c * faces + f) * 8, 8), :] for c in range(COMPS)]
        right = [right_ref[pl.ds((c * faces + f) * 8, 8), :] for c in range(COMPS)]
        flux = hllc(left, right, normal)
        if before is not None:
            for c in range(COMPS):
                emit(c, f - 1, flux[c] - before[c])
        before = flux


def half_lanes(shape):
    return lax.broadcasted_iota(jnp.int32, shape, 1) < 64


def swap_halves(x):
    return pltpu.roll(x, 64, 1)


def split3(x):
    hi = x.astype(BF16).astype(F32)
    mid = (x - hi).astype(BF16).astype(F32)
    return hi, mid, x - hi - mid


def fetch(source, target, sem, parts=1):
    step = -(-source.shape[0] // (parts * 16)) * 16
    for start in range(0, source.shape[0], step):
        rows = pl.ds(start, min(step, source.shape[0] - start))
        pltpu.make_async_copy(source.at[rows], target.at[rows], sem).start()
    return pltpu.make_async_copy(source, target, sem).wait


def pack_kernel(*refs):
    f_hbm, map_hbm, *sources = refs[:7]
    f_ref, r_ref, y1_ref, y2_ref, table_ref, *kept = refs[7:17]
    buf, map_ref, sems = refs[17:]
    pairs = [(f_hbm, f_ref, 8), (map_hbm, map_ref, 1)]
    pairs += list(zip(sources, kept, (1, 1, 8, 4, 1)))
    waits = [fetch(a, b, sems.at[i], parts) for i, (a, b, parts) in enumerate(pairs)]
    flags = place_flags()
    waits[0]()
    for x in range(8):
        def at(c):
            return f_ref[pl.ds(c * 64 + x * 8, 8), :]

        rho = at(0)
        inv = 1.0 / rho
        u = [at(c) * inv for c in (1, 2, 3)]
        p = (HEAT_RATIO - 1.0) * (
            at(4) - 0.5 * rho * (u[0] * u[0] + u[1] * u[1] + u[2] * u[2])
        )
        out = [jnp.log(rho)] + u + [jnp.log(p)] + [at(c) * inv for c in range(5, COMPS)]
        for c in range(COMPS):
            r_ref[pl.ds(c * 64 + x * 8, 8), :] = out[c]
    pushes = []
    for wall in range(2):
        rows = (0, 1, 2) if wall == 0 else (7, 6, 5)
        state = []
        for c in (0, 2, 4):
            a = [r_ref[pl.ds(c * 64 + y, 8, stride=8), :] for y in rows]
            sign = -1.0 if c == 2 else 1.0
            state.append(weno_one([a[2], a[1], a[0], sign * a[0], sign * a[1]]))
        rho = jnp.exp(state[0])
        p = jnp.exp(state[2])
        out_speed = -state[1] if wall == 0 else state[1]
        speed = jnp.abs(out_speed) + jnp.sqrt(HEAT_RATIO * p / rho)
        push = p + rho * out_speed * (out_speed + speed)
        x = jnp.where(flags[2 + wall], push, 0.0)
        for s in (1, 2, 4):
            x = x + pltpu.roll(x, 128 - s, 1)
        for s in (1, 2):
            x = x + pltpu.roll(x, 8 - s, 0)
        pushes.append(x)
    waits[1]()
    ids = map_ref[...].astype(F32)
    tall = jnp.concatenate(pushes + [ids, jnp.zeros((96, 128), F32)], axis=0)
    buf[...] = jnp.transpose(tall)
    groups = [buf[pl.ds(64 * g, 8, stride=8), :] for g in range(2)]
    lane = lax.broadcasted_iota(jnp.int32, (8, 128), 1).astype(F32)
    columns = []
    for g in groups:
        for col in (0, 4, 8, 12):
            columns.append(
                (
                    jnp.broadcast_to(g[:, col : col + 1], (8, 128)),
                    jnp.broadcast_to(g[:, 16 + col : 17 + col], (8, 128)),
                )
            )
    table = []
    for j in range(table_ref.shape[0]):
        total = jnp.zeros((8, 128), F32)
        for load, panel in columns:
            total = total + jnp.where(panel == lane + 128.0 * j, load, 0.0)
        table.append(jnp.sum(total, axis=0, keepdims=True))
        table_ref[pl.ds(j, 1), :] = table[j]
    for c in range(0, COMPS, 2):
        def row(i, y):
            return r_ref[pl.ds((c + i) * 64 + y, 8, stride=8), :]

        lo = jnp.concatenate([row(i, y) for i in (0, 1) for y in range(3)], axis=0)
        hi = jnp.concatenate([row(i, y) for i in (0, 1) for y in range(5, 8)], axis=0)
        store_layers((y1_ref, y2_ref), c, lo, hi, flags[7])
    rows = y1_ref.shape[0] - COMPS * 24
    pieces = [piece[j] for piece in zip(*map(split3, table)) for j in range(len(table))]
    if rows > len(pieces):
        pieces.append(jnp.zeros((rows - len(pieces), 128), F32))
    y1_ref[pl.ds(COMPS * 24, rows), :] = jnp.concatenate(pieces, axis=0).astype(BF16)
    for wait in waits[2:]:
        wait()


def store_layers(refs, c, lo, hi, parity):
    for m, ref in enumerate(refs):
        ref[pl.ds(c * 24, 48), :] = jnp.where(parity == m, hi, lo).astype(BF16)


def put_table_kernel(table_ref, x_ref, out_ref):
    start = COMPS * 24
    rows = x_ref.shape[0] - start
    pieces = list(split3(table_ref[...]))
    used = 3 * table_ref.shape[0]
    if rows > used:
        pieces.append(jnp.zeros((rows - used, 128), F32))
    out_ref[pl.ds(start, rows), :] = jnp.concatenate(pieces, axis=0).astype(BF16)


def put_table(table, x):
    return pl.pallas_call(
        put_table_kernel,
        out_shape=jax.ShapeDtypeStruct(x.shape, x.dtype),
        in_specs=[VM] * 2,
        out_specs=VM,
        input_output_aliases={1: 0},
        compiler_params=GRANT,
        cost_estimate=cost(0.2),
        name="put_table",
    )(table, x)


def in_hbm(x):
    return pltpu.with_memory_space_constraint(x, pltpu.HBM)


def load_rows(height):
    return -(-3 * height // 16) * 16


def pack(fields, panels, react, layers, height):
    whole = jax.ShapeDtypeStruct((COMPS * 64, 128), F32)
    outs = [whole, whole]
    outs.append(jax.ShapeDtypeStruct((COMPS * 24 + load_rows(height), 128), BF16))
    outs.append(jax.ShapeDtypeStruct((COMPS * 24, 128), BF16))
    outs.append(jax.ShapeDtypeStruct((height, 128), F32))
    one, two, three, four = layers
    kept = [jax.ShapeDtypeStruct(x.shape, x.dtype) for x in (react, one, two, three, four)]
    outs += kept
    return pl.pallas_call(
        pack_kernel,
        out_shape=outs,
        in_specs=[HBM] * 7,
        out_specs=[VM] * len(outs),
        scratch_shapes=[
            pltpu.VMEM((128, 128), F32),
            pltpu.VMEM(panels.shape, jnp.int32),
            pltpu.SemaphoreType.DMA((7,)),
        ],
        compiler_params=GRANT,
        cost_estimate=cost(2),
        name="pack",
    )(*map(in_hbm, (fields, panels, react, *layers)))


def turn_kernel(pair_x, r_ref, zt_ref, *refs):
    x_refs, (z1_ref, z2_ref, token) = refs[: 2 - pair_x], refs[2 - pair_x :]
    z_refs = (z1_ref, z2_ref)
    flags = place_flags()
    for c in range(0, COMPS, 2):
        lo = jnp.concatenate([r_ref[pl.ds((c + i) * 64, 24), :] for i in (0, 1)], axis=0)
        hi = jnp.concatenate([r_ref[pl.ds((c + i) * 64 + 40, 24), :] for i in (0, 1)], axis=0)
        store_layers(x_refs, c, lo, hi, flags[6])
    low = half_lanes((64, 128))
    for c in range(0, COMPS, 2):
        t = jnp.transpose(r_ref[pl.ds(c * 64, 128), :])
        top, bottom = t[:64], t[64:]
        even = jnp.where(low, top, swap_halves(bottom))
        odd = jnp.where(low, swap_halves(top), bottom)
        for i, x in ((0, even), (1, odd)):
            zt_ref[pl.ds((c + i) * 64, 64), :] = x
            for m, ref in enumerate(z_refs):
                up = flags[8] == m
                ref[pl.ds((c + i) * 3, 3), :] = jnp.where(up, x[61:], x[:3])
    for ref, start in [(x, COMPS * 24) for x in x_refs] + [(z, COMPS * 3) for z in z_refs]:
        if ref.shape[0] > start:
            ref[pl.ds(start, ref.shape[0] - start), :] = jnp.zeros(
                (ref.shape[0] - start, 128), ref.dtype
            )
    token[...] = jnp.zeros(token.shape, F32)


def turn(recon, pair_x, height):
    layer_x = jax.ShapeDtypeStruct((COMPS * 24 + (load_rows(height) if pair_x else 0), 128), BF16)
    edge = jax.ShapeDtypeStruct((40 + -(-height // 8) * 8, 128), F32)
    outs = [jax.ShapeDtypeStruct(recon.shape, F32)] + [layer_x] * (2 - pair_x) + [edge] * 2
    outs.append(jax.ShapeDtypeStruct((height, 128), F32))
    return pl.pallas_call(
        lambda *a: turn_kernel(int(pair_x), *a),
        out_shape=outs,
        in_specs=[VM],
        out_specs=[VM] * len(outs),
        compiler_params=GRANT,
        cost_estimate=cost(1),
        name="turn",
    )(recon)


def cost(us):
    return pl.CostEstimate(flops=0, transcendentals=0, bytes_accessed=int(us * 3.5e6))


def dot(a, b):
    return jnp.dot(a, b, preferred_element_type=F32)


def iota(shape, dim):
    return lax.broadcasted_iota(jnp.int32, shape, dim)


def where1(mask):
    return jnp.where(mask, 1.0, 0.0).astype(BF16)


def chem_in_kernel(
    slots, r_ref, react_ref, w1_ref, h_ref, row_ref, hit_ref, token
):
    react = react_ref[...].astype(F32)
    react_b = react.astype(BF16)
    upper = where1(iota((128, 128), 0) <= iota((128, 128), 1))
    within = dot(react_b, upper)
    count = dot(react_b, jnp.ones((128, 128), BF16))
    below = where1(iota((64, 64), 1) < iota((64, 64), 0))
    offset = dot(below, count.astype(BF16))
    rank = (react * (within + offset)).astype(BF16)
    slot_lane = iota((64, slots), 1).astype(F32)
    off_col, cnt_col = offset[:, :1], count[:, :1]
    row_ref[...] = where1((slot_lane >= off_col) & (slot_lane < off_col + cnt_col))
    nt = (((1,), (1,)), ((), ()))
    count_row = lax.dot_general(
        jnp.ones((8, 128), BF16), react_b, nt, preferred_element_type=F32
    )
    offset_row = lax.dot_general(
        count_row.astype(BF16), below, nt, preferred_element_type=F32
    )
    slot_sub = iota((slots, 64), 0).astype(F32)
    slot_row = where1(
        (slot_sub >= offset_row[:1]) & (slot_sub < offset_row[:1] + count_row[:1])
    )
    lane_hit = dot(slot_row, rank) == iota((slots, 128), 0).astype(F32) + 1.0
    hit_ref[...] = where1(lane_hit)
    feat = jnp.zeros((slots, 128), F32)
    for c in range(COMPS):
        rows = dot(slot_row, r_ref[pl.ds(c * 64, 64), :].astype(BF16))
        hit = jnp.where(lane_hit, rows, 0.0).astype(BF16)
        feat = feat + dot(hit, where1(iota((128, 128), 1) == c))
    feat = jnp.transpose(feat)[:COMPS].astype(BF16)
    tn = (((0,), (0,)), ((), ()))
    one = lax.dot_general(w1_ref[...], feat, tn, preferred_element_type=F32)
    h_ref[...] = jax.nn.gelu(one).astype(BF16)
    token[...] = jnp.zeros(token.shape, F32)


def chem_in(recon, react, layer_one, slots, table):
    return pl.pallas_call(
        lambda *a: chem_in_kernel(slots, *a),
        out_shape=[
            jax.ShapeDtypeStruct((layer_one.shape[1], slots), BF16),
            jax.ShapeDtypeStruct((64, slots), BF16),
            jax.ShapeDtypeStruct((slots, 128), BF16),
            token_shape(table),
        ],
        in_specs=[VM] * 3,
        out_specs=[VM] * 4,
        compiler_params=GRANT,
        cost_estimate=cost(1),
        name="chem_in",
    )(recon, react, layer_one)


def chem_mid_kernel(h_ref, w2_ref, w3_ref, out_ref, token):
    two = jax.nn.gelu(dot(w2_ref[...], h_ref[...])).astype(BF16)
    out_ref[...] = jax.nn.gelu(dot(w3_ref[...], two)).astype(BF16)
    token[...] = jnp.zeros(token.shape, F32)


def chem_mid(hidden, layer_two, layer_three, table):
    return pl.pallas_call(
        chem_mid_kernel,
        out_shape=[
            jax.ShapeDtypeStruct((layer_three.shape[0], hidden.shape[1]), BF16),
            token_shape(table),
        ],
        in_specs=[VM] * 3,
        out_specs=[VM] * 2,
        compiler_params=GRANT,
        cost_estimate=cost(2),
        name="chem_mid",
    )(hidden, layer_two, layer_three)


def chem_out_kernel(h_ref, w4_ref, row_ref, hit_ref, out_ref, token):
    rates = dot(w4_ref[...], h_ref[...])
    slots = rates.shape[1]
    rates = jnp.concatenate([rates, jnp.zeros((128 - COMPS, slots), F32)], axis=0)
    rates_t = jnp.transpose(rates).astype(BF16)
    hit, row_slot = hit_ref[...].astype(F32), row_ref[...]
    for c in range(COMPS):
        spread = hit * dot(rates_t, where1(iota((128, 128), 0) == c))
        out_ref[pl.ds(c * 64, 64), :] = dot(row_slot, spread.astype(BF16))
    token[...] = jnp.zeros(token.shape, F32)


def chem_out(hidden, layer_four, row_slot, hit, table):
    return pl.pallas_call(
        chem_out_kernel,
        out_shape=[jax.ShapeDtypeStruct((COMPS * 64, 128), F32), token_shape(table)],
        in_specs=[VM] * 4,
        out_specs=[VM] * 2,
        compiler_params=GRANT,
        cost_estimate=cost(1),
        name="chem_out",
    )(hidden, layer_four, row_slot, hit)


def halo_lines(refs, scratch, own, sign_comp, at_wall, order, second):
    for c in range(0, COMPS, 2):
        block = refs[0][pl.ds(c * 24, 48), :].astype(F32)
        if len(refs) == 2:
            block = jnp.where(second, refs[1][pl.ds(c * 24, 48), :].astype(F32), block)
        for i in (0, 1):
            for k in range(3):
                mirror = own(c + i, order[k])
                if c + i == sign_comp:
                    mirror = -mirror
                got = block[(i * 3 + k) * 8 : (i * 3 + k + 1) * 8]
                scratch[pl.ds(((c + i) * 3 + k) * 8, 8), :] = jnp.where(at_wall, mirror, got)


def flux_x_kernel(count, f_ref, r_ref, acc_ref, src_ref, *refs):
    flags = place_flags()
    layers, (out_hbm, lo_s, hi_s, left, right, out_ref, sems) = refs[:count], refs[count:]

    def own(c, x):
        return r_ref[pl.ds(c * 64 + x * 8, 8), :]

    halo_lines(layers, lo_s, own, 1, flags[0], (2, 1, 0), flags[6] == 0)
    halo_lines(layers, hi_s, own, 1, flags[1], (7, 6, 5), flags[6] == 1)

    def line(c):
        return (
            [lo_s[rows8(c * 3 + k), :] for k in range(3)]
            + [r_ref[rows8(c * 8 + x), :] for x in range(8)]
            + [hi_s[rows8(c * 3 + k), :] for k in range(3)]
        )

    face_states(line, left, right, 9)
    copies = []

    def emit(c, x, change):
        at, plane = pl.ds(c * 64 + x * 8, 8), pl.ds(x * 8, 8)
        new = f_ref[at, :] - TIME_STEP * (acc_ref[at, :] + change) + CHEM_STEP * src_ref[at, :]
        out_ref[c, plane, :] = new
        if c == COMPS - 1:
            here, there = out_ref.at[:, plane], out_hbm.at[:, plane]
            copies.append(pltpu.make_async_copy(here, there, sems.at[x]))
            copies[-1].start()

    line_changes(left, right, 9, 0, emit)
    for copy in copies:
        copy.wait()


def flux_y_kernel(count, r_ref, *refs):
    flags = place_flags()
    layers, (out_ref, token, lo_s, hi_s, left, right) = refs[:count], refs[count:]

    def own(c, y):
        return r_ref[pl.ds(c * 64 + y, 8, stride=8), :]

    halo_lines(layers, lo_s, own, 2, flags[2], (2, 1, 0), flags[7] == 0)
    halo_lines(layers, hi_s, own, 2, flags[3], (7, 6, 5), flags[7] == 1)

    def line(c):
        return (
            [lo_s[rows8(c * 3 + k), :] for k in range(3)]
            + [r_ref[pl.ds(c * 64 + y, 8, stride=8), :] for y in range(8)]
            + [hi_s[rows8(c * 3 + k), :] for k in range(3)]
        )

    face_states(line, left, right, 9)

    def emit(c, y, change):
        out_ref[pl.ds(c * 64 + y, 8, stride=8), :] = change

    line_changes(left, right, 9, 1, emit)
    token[...] = jnp.zeros(token.shape, F32)


def flux_z_kernel(count, zt_ref, acc_ref, *refs):
    flags = place_flags()
    layers, (out_ref, token, ext, left, right, back) = refs[:count], refs[count:]
    low3, low = half_lanes((3, 128)), half_lanes((64, 128))

    def got(c, second):
        x = layers[0][pl.ds(c * 3, 3), :]
        if count == 2:
            x = jnp.where(second, layers[1][pl.ds(c * 3, 3), :], x)
        return swap_halves(x)

    for c in range(COMPS):
        sign = -1.0 if c == 3 else 1.0
        own = zt_ref[pl.ds(c * 64, 64), :]
        first, last = own[:3], own[61:]
        mirror_lo = sign * jnp.concatenate([first[2:3], first[1:2], first[0:1]], axis=0)
        mirror_hi = sign * jnp.concatenate([last[2:3], last[1:2], last[0:1]], axis=0)
        below = jnp.where(flags[4], mirror_lo, got(c, flags[8] == 0))
        above = jnp.where(flags[5], mirror_hi, got(c, flags[8] == 1))
        ext[pl.ds(c * 72, 3), :] = jnp.where(low3, below, swap_halves(last))
        ext[pl.ds(c * 72 + 3, 64), :] = own
        ext[pl.ds(c * 72 + 67, 3), :] = jnp.where(low3, swap_halves(first), above)

    def line(c):
        return [ext[pl.ds(c * 72 + e, 8, stride=8), :] for e in range(14)]

    face_states(line, left, right, 9)

    def emit(c, z, change):
        back[pl.ds(c * 64 + z, 8, stride=8), :] = change

    line_changes(left, right, 9, 2, emit)
    for c in range(0, COMPS, 2):
        even, odd = back[pl.ds(c * 64, 64), :], back[pl.ds(c * 64 + 64, 64), :]
        t = jnp.concatenate(
            [jnp.where(low, even, swap_halves(odd)), jnp.where(low, swap_halves(even), odd)],
            axis=0,
        )
        at = pl.ds(c * 64, 128)
        out_ref[at, :] = acc_ref[at, :] + jnp.transpose(t)
    token[...] = jnp.zeros(token.shape, F32)


def impulse_kernel(own, table_ref, got_ref, out_ref):
    place = place_flags()[9] * own
    row = pl.ds(place // 128, 1)
    loads = jnp.broadcast_to(table_ref[row, :] + got_ref[row, :], (8, 128))
    loads = pltpu.roll(loads, (128 - place % 128) % 128, 1)
    out_ref[...] = loads[:1, :own] * (1.0 / (PATCH * PATCH))


def own_impulse(table, got, own):
    return pl.pallas_call(
        lambda *a: impulse_kernel(own, *a),
        out_shape=jax.ShapeDtypeStruct((1, own), F32),
        in_specs=[VM] * 2,
        out_specs=VM,
        compiler_params=GRANT,
        cost_estimate=cost(0.5),
        name="impulse",
    )(table, got)


def state_scratch():
    return [pltpu.VMEM((COMPS * 9 * 8, 128), F32)] * 2


def halo_scratch():
    return [pltpu.VMEM((COMPS * 24, 128), F32)] * 2


def token_shape(table):
    return jax.ShapeDtypeStruct(table.shape, F32)


def flux_x(fields, recon, acc, source, layers):
    return pl.pallas_call(
        lambda *a: flux_x_kernel(len(layers), *a),
        out_shape=jax.ShapeDtypeStruct((COMPS, 64, 128), F32),
        in_specs=[VM] * (4 + len(layers)),
        out_specs=HBM,
        scratch_shapes=halo_scratch()
        + state_scratch()
        + [pltpu.VMEM((COMPS, 64, 128), F32), pltpu.SemaphoreType.DMA((8,))],
        compiler_params=GRANT,
        cost_estimate=cost(2),
        name="flux_x",
    )(fields, recon, acc, source, *layers)


def flux_y(recon, layers, table):
    return pl.pallas_call(
        lambda *a: flux_y_kernel(len(layers), *a),
        out_shape=[jax.ShapeDtypeStruct(recon.shape, F32), token_shape(table)],
        in_specs=[VM] * (1 + len(layers)),
        out_specs=[VM] * 2,
        scratch_shapes=halo_scratch() + state_scratch(),
        compiler_params=GRANT,
        cost_estimate=cost(2),
        name="flux_y",
    )(recon, *layers)


def flux_z(turned, acc, layers, table):
    return pl.pallas_call(
        lambda *a: flux_z_kernel(len(layers), *a),
        out_shape=[jax.ShapeDtypeStruct(acc.shape, F32), token_shape(table)],
        in_specs=[VM] * (2 + len(layers)),
        out_specs=[VM] * 2,
        scratch_shapes=[pltpu.VMEM((COMPS * 72, 128), F32)]
        + state_scratch()
        + [pltpu.VMEM(acc.shape, F32)],
        compiler_params=GRANT,
        cost_estimate=cost(2),
        name="flux_z",
    )(turned, acc, *layers)


def swap(x, axis, second, outer=False):
    n = lax.axis_size(axis)
    pairs = [(i, i + 1) for i in range(int(second), n - 1, 2)]
    if outer:
        pairs.append((0, n - 1))
    return lax.ppermute(x, axis, [(a, b) for a, b in pairs] + [(b, a) for a, b in pairs])


def swap_inner(x, axis, other):
    n, m = lax.axis_size(axis), lax.axis_size(other)
    if m % 2 or n % 2:
        return swap(x, axis, 1)
    pairs = []
    for i in range(n):
        for j in range(m):
            end = i in (0, n - 1)
            to = (i, j ^ 1) if end else (i + 1 if i % 2 else i - 1, j)
            pairs.append((i * m + j, to[0] * m + to[1]))
    return lax.ppermute(x, (axis, other), pairs)


def sum_over(table, axis, step=1):
    size = lax.axis_size(axis)
    if size & (size - 1):
        return lax.psum(table, axis)
    while step < size:
        table = table + lax.ppermute(table, axis, [(i, i ^ step) for i in range(size)])
        step *= 2
    return table


def join_table(rows, height):
    rows = rows[: 3 * height].astype(F32)
    return rows[:height] + rows[height : 2 * height] + rows[2 * height :]


def body(fields, reacting, panel_map, layer_one, layer_two, layer_three, layer_four):
    shape = fields.shape
    sizes = [lax.axis_size(a) for a in AXES]
    pair_x = sizes[0] == 2
    panels_all = 2 * (shape[1] * sizes[0] // PATCH) * (shape[3] * sizes[2] // PATCH)
    own = panels_all // (sizes[0] * sizes[1] * sizes[2])
    height = panels_all // 128
    slots = BAL * min(4, sizes[0])
    layer_rows, edge_rows = COMPS * 24, 40
    ride_y, ride_z = sizes[1] & (sizes[1] - 1) == 0, sizes[2] in (2, 4)

    flat = fields.reshape(-1, shape[3])
    panels, react = panel_map.reshape(-1, shape[3]), reacting.reshape(-1, shape[3])
    layers = (layer_one.T, layer_two, layer_three, layer_four)
    packed = pack(flat, panels, react, layers, height)
    flat, recon, y_first, y_second, table, react, one, two, three, four = packed
    y_got = [swap(y_first, "gy", 0)]
    if sizes[1] > 2:
        y_got.append(swap_inner(y_second, "gy", "gz"))
    turned, *xs, z_first, z_second, token = turn(recon, pair_x, height)
    hidden, row_slot, hit, token_in = chem_in(recon, react, one, slots, table)
    table = table + token + token_in
    if ride_y:
        table = table + join_table(y_got[0][layer_rows:], height)
    if not ride_z:
        table = sum_over(table, "gz")
    z_got = [swap(lax.dynamic_update_slice(z_first, table, (edge_rows, 0)), "gz", 0)]
    hidden, token = chem_mid(hidden, two, three, table)
    if ride_z:
        table = table + z_got[0][edge_rows : edge_rows + height] + token
    if sizes[2] > 2:
        z_second = lax.dynamic_update_slice(z_second, table, (edge_rows, 0))
        z_got.append(swap(z_second, "gz", 1, ride_z))
        if ride_z:
            table = table + z_got[1][edge_rows : edge_rows + height]
    acc, token = flux_y(recon, y_got, table)
    table = table + token
    if pair_x:
        xs = [put_table(table, xs[0])]
    x_got = [swap(x, "gx", m) for m, x in enumerate(xs)]
    acc, token = flux_z(turned, acc, z_got, table)
    source, token_out = chem_out(hidden, four, row_slot, hit, table)
    table = table + token + token_out
    if pair_x:
        table = table + join_table(x_got[0][layer_rows:], height)
    else:
        table = sum_over(table, "gx")
    rest = jnp.zeros_like(table)
    if not ride_y:
        table = lax.psum(table, "gy")
    elif sizes[1] > 2:
        table = sum_over(table, "gy", 4)
        pairs = [(i, i ^ 2) for i in range(sizes[1])]
        rest = lax.ppermute(table, "gy", pairs)
    new = flux_x(flat, recon, acc, source, x_got)
    return new.reshape(shape), own_impulse(table, rest, own).reshape(own)


def solution(mesh):
    return jax.shard_map(
        body,
        mesh=mesh,
        in_specs=(
            P(None, "gx", "gy", "gz"),
            P("gx", "gy", "gz"),
            P(None, "gx", "gz"),
            P(),
            P(),
            P(),
            P(),
        ),
        out_specs=(P(None, "gx", "gy", "gz"), P(("gx", "gy", "gz"))),
        check_vma=False,
    )
```

profile of v0, /device:TPU:0, one launch (start us, length us, event | category | flops | bytes accessed | tf_op | source)
XLA Modules:
  0.0 24.6 jit_solution(4784187084627110897)
XLA Ops:
  0.6 2.2 %pack.1 = (f32[768,128]{1,0:T(8,128)S(1)}, f32[768,128]{1,0:T(8,128)S(1)}, bf16[304,128]{1,0:T(8,128)(2,1)S(1)}, bf16[288,128]{1,0:T(8,128)(2,1)S(1)}, f32[2,128...) custom-call(f32[768,128]{1,0:T(8,128)} %bitcast.6, ...), custom_call_target="tpu_custom_call" | custom-call | bytes 7000000 | tf_op jit(solution)/shard_map/pack/pallas_call | solution.py:286
  2.8 3.1 %collective-permute-start = (bf16[304,128]{1,0:T(8,128)(2,1)S(1)}, bf16[304,128]{1,0:T(8,128)(2,1)S(1)}, u32[]{:S(2)}, u32[]{:S(2)}) collective-permute-start(bf16[304,128]{1,0:T(8,128)(2,1)S(1)} %get-tuple-element.32), channel_id=1, source_target_pairs={{0,4},{8,12},{4,0},{12,8},{1,5},{9,13},{5,1},{13,9},{2,6},{10,14},... | collective-permute-start | bytes 233480 | tf_op jit(solution)/shard_map/ppermute | solution.py:659
  6.0 0.3 %turn.1 = (f32[768,128]{1,0:T(8,128)S(1)}, bf16[304,128]{1,0:T(8,128)(2,1)S(1)}, f32[48,128]{1,0:T(8,128)S(1)}, f32[48,128]{1,0:T(8,128)S(1)}, f32[2,128]{1,0:T(2,128)S(1)}) custom-call(f32[768,128]{1,0:T(8,128)S(1)} %get-tuple-element.30.a_0_.a_1_), custom_call_target="tpu_custom_call" | custom-call | bytes 3500000 | tf_op jit(solution)/shard_map/turn/pallas_call | solution.py:334
  6.3 1.2 %chem_in.1 = (bf16[1600,128]{1,0:T(8,128)(2,1)S(1)}, bf16[64,128]{1,0:T(8,128)(2,1)S(1)}, bf16[128,128]{1,0:T(8,128)(2,1)S(1)}, f32[2,128]{1,0:T(2,128)S(1)}) custom-call(f32[768,128]{1,0:T(8,128)S(1)} %get-tuple-element.30.a_0_.a_1_, s32[64,128]{1,0:T(8,128)S(1)} %get-tuple-element.38.a_1_, bf16[12,1600]{1,0:T(8,128)(2,1)S(1)} %get-tuple-element.39.a_2_), custom_call_target="tpu_custom_call" | custom-call | bytes 3500000 | tf_op jit(solution)/shard_map/chem_in/pallas_call | solution.py:401
  7.5 0.8 %collective-permute-done.a_1_ = bf16[304,128]{1,0:T(8,128)(2,1)S(1)} collective-permute-done((bf16[304,128]{1,0:T(8,128)(2,1)S(1)}, bf16[304,128]{1,0:T(8,128)(2,1)S(1)}, u32[]{:S(2)}, u32[]{:S(2)}) %collective-permute-start) | collective-permute-done | bytes 77856 | tf_op jit(solution)/shard_map/ppermute | solution.py:659
  8.4 0.1 collective-permute-start.2
  8.4 0.5 %collective-permute-start.1 = (bf16[288,128]{1,0:T(8,128)(2,1)S(1)}, bf16[288,128]{1,0:T(8,128)(2,1)S(1)}, u32[]{:S(2)}, u32[]{:S(2)}) collective-permute-start(bf16[288,128]{1,0:T(8,128)(2,1)S(1)} %get-tuple-element.33), channel_id=1, source_target_pairs={{0,1},{1,0},{2,3},{3,2},{4,8},{5,9},{6,10},{7,11},{8,4},{9,5},{10,... | collective-permute-start | bytes 221192 | tf_op jit(solution)/shard_map/ppermute | solution.py:672
  8.9 1.5 %chem_mid.1 = (bf16[400,128]{1,0:T(8,128)(2,1)S(1)}, f32[2,128]{1,0:T(2,128)S(1)}) custom-call(bf16[1600,128]{1,0:T(8,128)(2,1)S(1)} %get-tuple-element.42.h_ref, bf16[800,1600]{1,0:T(8,128)(2,1)S(1)} %get-tuple-element.43.w2_ref, bf16[400,800]{1,0:T(8,128)(2,1)S(1)} %get-tuple-element.44.w3_ref), custom_call_target="tpu_custom_call" | custom-call | bytes 7000000 | tf_op jit(solution)/shard_map/chem_mid/pallas_call | solution.py:424
  10.4 0.0 collective-permute-done.2.a_2_
  10.4 1.7 %collective-permute-start.3 = (f32[48,128]{1,0:T(8,128)S(1)}, f32[48,128]{1,0:T(8,128)S(1)}, u32[]{:S(2)}, u32[]{:S(2)}) collective-permute-start(f32[48,128]{1,0:T(8,128)S(1)} %constant_dynamic-update-slice_fusion), channel_id=1, source_target_pairs={{1,2},{0,3},{2,1},{3,0},{5,6},{4,7},{6,5},{7,4},{9,10},{8,11},{10,... | collective-permute-start | bytes 73736 | tf_op jit(solution)/shard_map/ppermute | solution.py:659
  12.1 0.0 collective-permute-done.1.a_2_
  12.2 1.3 %flux_y.1 = (f32[768,128]{1,0:T(8,128)S(1)}, f32[2,128]{1,0:T(2,128)S(1)}) custom-call(f32[768,128]{1,0:T(8,128)S(1)} %get-tuple-element.30.a_0_.a_1_, bf16[304,128]{1,0:T(8,128)(2,1)S(1)} %collective-permute-done.a_1_, bf16[288,128]{1,0:T(8,128)(2,1)S(1)} %collective-permute-done.1.a_2_), custom_call_target="tpu_custom_call" | custom-call | bytes 7000000 | tf_op jit(solution)/shard_map/flux_y/pallas_call | solution.py:627
  13.4 0.3 %collective-permute-done.3.a_3_ = f32[48,128]{1,0:T(8,128)S(1)} collective-permute-done((f32[48,128]{1,0:T(8,128)S(1)}, f32[48,128]{1,0:T(8,128)S(1)}, u32[]{:S(2)}, u32[]{:S(2)}) %collective-permute-start.3) | collective-permute-done | bytes 24608 | tf_op jit(solution)/shard_map/ppermute | solution.py:659
  13.8 2.0 %collective-permute-start.4 = (bf16[304,128]{1,0:T(8,128)(2,1)S(1)}, bf16[304,128]{1,0:T(8,128)(2,1)S(1)}, u32[]{:S(2)}, u32[]{:S(2)}) collective-permute-start(bf16[304,128]{1,0:T(8,128)(2,1)S(1)} %put_table.1), channel_id=1, source_target_pairs={{0,16},{16,0},{1,17},{17,1},{2,18},{18,2},{3,19},{19,3},{4,20},{20... | collective-permute-start | bytes 233480 | tf_op jit(solution)/shard_map/ppermute | solution.py:659
  15.8 0.7 %chem_out.1 = (f32[768,128]{1,0:T(8,128)S(1)}, f32[2,128]{1,0:T(2,128)S(1)}) custom-call(bf16[400,128]{1,0:T(8,128)(2,1)S(1)} %get-tuple-element.47.h_ref, bf16[12,400]{1,0:T(8,128)(2,1)S(1)} %get-tuple-element.48.w4_ref, bf16[64,128]{1,0:T(8,128)(2,1)S(1)} %get-tuple-element.49.row_ref, bf16[128,128]{1,0:T(8,128)(2,1)S(1)} %get-tuple-element.50.hit_ref), custom_call_target="tpu_custom_call" | custom-call | bytes 3500000 | tf_op jit(solution)/shard_map/chem_out/pallas_call | solution.py:451
  16.4 1.5 %flux_z.1 = (f32[768,128]{1,0:T(8,128)S(1)}, f32[2,128]{1,0:T(2,128)S(1)}) custom-call(f32[768,128]{1,0:T(8,128)S(1)} %get-tuple-element.31.a_0_, f32[768,128]{1,0:T(8,128)S(1)} %get-tuple-element.34.a_1_, f32[48,128]{1,0:T(8,128)S(1)} %collective-permute-done.2.a_2_, f32[48,128]{1,0:T(8,128)S(1)} %collective-permute-done.3.a_3_), custom_call_target="tpu_custom_call" | custom-call | bytes 7000000 | tf_op jit(solution)/shard_map/flux_z/pallas_call | solution.py:640
  18.0 0.5 %collective-permute-done.4.a_4_ = bf16[304,128]{1,0:T(8,128)(2,1)S(1)} collective-permute-done((bf16[304,128]{1,0:T(8,128)(2,1)S(1)}, bf16[304,128]{1,0:T(8,128)(2,1)S(1)}, u32[]{:S(2)}, u32[]{:S(2)}) %collective-permute-start.4) | collective-permute-done | bytes 77856 | tf_op jit(solution)/shard_map/ppermute | solution.py:659
  18.4 3.5 %collective-permute-start.5 = (f32[2,128]{1,0:T(2,128)S(1)}, f32[2,128]{1,0:T(2,128)S(1)}, u32[]{:S(2)}, u32[]{:S(2)}) collective-permute-start(f32[2,128]{1,0:T(2,128)S(1)} %add_add_fusion.a_0_), channel_id=1, source_target_pairs={{0,8},{4,12},{8,0},{12,4},{1,9},{5,13},{9,1},{13,5},{2,10},{6,14},... | collective-permute-start | bytes 3080 | tf_op jit(solution)/shard_map/ppermute | solution.py:743
  22.0 1.9 %flux_x.1 = f32[12,64,128]{2,1,0:T(8,128)} custom-call(f32[768,128]{1,0:T(8,128)S(1)} %get-tuple-element.29.a_0_, f32[768,128]{1,0:T(8,128)S(1)} %get-tuple-element.30.a_0_.a_1_, f32[768,128]{1,0:T(8,128)S(1)} %get-tuple-element.46.a_2_, f32[768,128]{1,0:T(8,128)S(1)} %get-tuple-element.51.a_3_, bf16[304,128]{1,0:T(8,128)(2,1)S(1)} %collective-permute-done.4.a_4_), custom_call_target="tpu_custom_call" | custom-call | bytes 7000000 | tf_op jit(solution)/shard_map/flux_x/pallas_call | solution.py:612
  23.9 0.0 collective-permute-done.5.a_1_
  24.0 0.6 %impulse.1 = f32[1,8]{1,0:T(1,128)} custom-call(f32[2,128]{1,0:T(2,128)S(1)} %add_add_fusion.a_0_, f32[2,128]{1,0:T(2,128)S(1)} %collective-permute-done.5.a_1_), custom_call_target="tpu_custom_call" | custom-call | bytes 1750000 | tf_op jit(solution)/shard_map/impulse/pallas_call | solution.py:588
  (7 shorter events, 0.1 us)
Async XLA Ops:
  2.8 5.5 %collective-permute-start = (bf16[304,128]{1,0:T(8,128)(2,1)S(1)}, bf16[304,128]{1,0:T(8,128)(2,1)S(1)}, u32[]{:S(2)}, u32[]{:S(2)}) collective-permute-start(bf16[304,128]{1,0:T(8,128)(2,1)S(1)} %get-tuple-element.32), channel_id=1, source_target_pairs={{0,4},{8,12},{4,0},{12,8},{1,5},{9,13},{5,1},{13,9},{2,6},{10,14},... | collective-permute-start | bytes 233480 | tf_op jit(solution)/shard_map/ppermute | solution.py:659
  8.4 2.1 %collective-permute-start.2 = (f32[48,128]{1,0:T(8,128)S(1)}, f32[48,128]{1,0:T(8,128)S(1)}, u32[]{:S(2)}, u32[]{:S(2)}) collective-permute-start(f32[48,128]{1,0:T(8,128)S(1)} %get-tuple-element.56), channel_id=1, source_target_pairs={{0,1},{2,3},{1,0},{3,2},{4,5},{6,7},{5,4},{7,6},{8,9},{10,11},{9,8... | collective-permute-start | bytes 73736 | tf_op jit(solution)/shard_map/ppermute | solution.py:659
  8.4 3.7 %collective-permute-start.1 = (bf16[288,128]{1,0:T(8,128)(2,1)S(1)}, bf16[288,128]{1,0:T(8,128)(2,1)S(1)}, u32[]{:S(2)}, u32[]{:S(2)}) collective-permute-start(bf16[288,128]{1,0:T(8,128)(2,1)S(1)} %get-tuple-element.33), channel_id=1, source_target_pairs={{0,1},{1,0},{2,3},{3,2},{4,8},{5,9},{6,10},{7,11},{8,4},{9,5},{10,... | collective-permute-start | bytes 221192 | tf_op jit(solution)/shard_map/ppermute | solution.py:672
  10.4 3.3 %collective-permute-start.3 = (f32[48,128]{1,0:T(8,128)S(1)}, f32[48,128]{1,0:T(8,128)S(1)}, u32[]{:S(2)}, u32[]{:S(2)}) collective-permute-start(f32[48,128]{1,0:T(8,128)S(1)} %constant_dynamic-update-slice_fusion), channel_id=1, source_target_pairs={{1,2},{0,3},{2,1},{3,0},{5,6},{4,7},{6,5},{7,4},{9,10},{8,11},{10,... | collective-permute-start | bytes 73736 | tf_op jit(solution)/shard_map/ppermute | solution.py:659
  13.8 4.7 %collective-permute-start.4 = (bf16[304,128]{1,0:T(8,128)(2,1)S(1)}, bf16[304,128]{1,0:T(8,128)(2,1)S(1)}, u32[]{:S(2)}, u32[]{:S(2)}) collective-permute-start(bf16[304,128]{1,0:T(8,128)(2,1)S(1)} %put_table.1), channel_id=1, source_target_pairs={{0,16},{16,0},{1,17},{17,1},{2,18},{18,2},{3,19},{19,3},{4,20},{20... | collective-permute-start | bytes 233480 | tf_op jit(solution)/shard_map/ppermute | solution.py:659
  18.4 5.5 %collective-permute-start.5 = (f32[2,128]{1,0:T(2,128)S(1)}, f32[2,128]{1,0:T(2,128)S(1)}, u32[]{:S(2)}, u32[]{:S(2)}) collective-permute-start(f32[2,128]{1,0:T(2,128)S(1)} %add_add_fusion.a_0_), channel_id=1, source_target_pairs={{0,8},{4,12},{8,0},{12,4},{1,9},{5,13},{9,1},{13,5},{2,10},{6,14},... | collective-permute-start | bytes 3080 | tf_op jit(solution)/shard_map/ppermute | solution.py:743
where the time goes:
time: 24.7 us; the launch traced here: 24.6 us
  Pallas kernels  11.3 us (46%)
  starting transfers between devices  10.9 us (44%)
  waiting for transfers between devices  1.59 us (6%)
  between operations  0.71 us (3%)
    ppermute x4, starting transfers between devices, swap(): lax.ppermute(x, axis, [(a, b) for a, b in pairs] + [(b, a) for a, b in pa...  6.89 us
    ppermute x1, starting transfers between devices, body(): rest = lax.ppermute(table, 'gy', pairs)  3.54 us
    pallas_call x1, Pallas kernels, pack(): pl.pallas_call(pack_kernel, out_shape=outs, in_specs=[HBM] * 7, out_specs...  2.2 us
    pallas_call x1, Pallas kernels, flux_x(): pl.pallas_call(lambda *a: flux_x_kernel(len(layers), *a), out_shape=jax.S...  1.94 us
    ppermute x4, waiting for transfers between devices, swap(): lax.ppermute(x, axis, [(a, b) for a, b in pairs] + [(b, a) for a, b in pa...  1.58 us
    pallas_call x1, Pallas kernels, flux_z(): pl.pallas_call(lambda *a: flux_z_kernel(len(layers), *a), out_shape=[jax....  1.54 us
    pallas_call x1, Pallas kernels, chem_mid(): pl.pallas_call(chem_mid_kernel, out_shape=[jax.ShapeDtypeStruct((layer_th...  1.48 us
    pallas_call x1, Pallas kernels, flux_y(): pl.pallas_call(lambda *a: flux_y_kernel(len(layers), *a), out_shape=[jax....  1.26 us
  transfers between devices with their start and end apart: 6, of which 3 were waited for; matrix products, arithmetic and copies ran while one was open for 0% of the time, Pallas kernels for 34%

commit v1 on v0

--- a/solution.py
+++ b/solution.py
@@ -23,16 +23,17 @@
 HBM = pl.BlockSpec(memory_space=pltpu.HBM)
 
 
-def weno_line(v):
+def weno_line(v, first, last):
     n = len(v)
-    d = [(v[j + 1] - v[j]) * (1.0 / 6.0) for j in range(n - 1)]
-    d3 = [3.0 * x for x in d]
+    low, high = max(first - 2, 0), min(last + 2, n - 1)
+    d = {j: (v[j + 1] - v[j]) * (1.0 / 6.0) for j in range(low, high)}
+    d3 = {j: 3.0 * d[j] for j in range(low + 1, high - 1)}
     q = {}
-    for e in range(1, n - 1):
+    for e in range(low + 1, high):
         s = d[e] - d[e - 1]
         q[e] = (13.0 / 3.0) * (s * s) + EPS
     upper, lower = {}, {}
-    for e in range(2, n - 2):
+    for e in range(first, last + 1):
         dm, dp = d[e - 1], d[e]
         t0 = d3[e - 1] - d[e - 2]
         t1 = dm + dp
@@ -114,23 +115,30 @@
     return pl.ds(pl.multiple_of(index * 8, 8), 8)
 
 
-def face_states(load_line, left_ref, right_ref, faces):
+def face_states(load_line, left_ref, right_ref, faces, spans=((2, 11),)):
     def one(c, carry):
-        upper, lower = weno_line(load_line(c))
-        for f in range(faces):
-            left_ref[rows8(c * faces + f), :] = upper[f + 2]
-            right_ref[rows8(c * faces + f), :] = lower[f + 3]
+        line = load_line(c)
+        for first, last in spans:
+            upper, lower = weno_line(line, first, last)
+            for e, x in upper.items():
+                left_ref[rows8(c * faces + e - 2), :] = x
+            for e, x in lower.items():
+                right_ref[rows8(c * faces + e - 3), :] = x
         return carry
 
     lax.fori_loop(0, COMPS, one, 0)
+
+
+def face_flux(left_ref, right_ref, faces, normal, f):
+    left = [left_ref[pl.ds((c * faces + f) * 8, 8), :] for c in range(COMPS)]
+    right = [right_ref[pl.ds((c * faces + f) * 8, 8), :] for c in range(COMPS)]
+    return hllc(left, right, normal)
 
 
 def line_changes(left_ref, right_ref, faces, normal, emit):
     before = None
     for f in range(faces):
-        left = [left_ref[pl.ds((c * faces + f) * 8, 8), :] for c in range(COMPS)]
-        right = [right_ref[pl.ds((c * faces + f) * 8, 8), :] for c in range(COMPS)]
-        flux = hllc(left, right, normal)
+        flux = face_flux(left_ref, right_ref, faces, normal, f)
         if before is not None:
             for c in range(COMPS):
                 emit(c, f - 1, flux[c] - before[c])
@@ -414,25 +422,32 @@
     )(recon, react, layer_one)
 
 
-def chem_mid_kernel(h_ref, w2_ref, w3_ref, out_ref, token):
-    two = jax.nn.gelu(dot(w2_ref[...], h_ref[...])).astype(BF16)
+def chem_two_kernel(h_ref, w2_ref, out_ref, token):
+    half = out_ref.shape[0]
+    out_ref[...] = jax.nn.gelu(dot(w2_ref[pl.ds(0, half), :], h_ref[...])).astype(BF16)
+    token[...] = jnp.zeros(token.shape, F32)
+
+
+def chem_three_kernel(h_ref, two_ref, w2_ref, w3_ref, out_ref, token):
+    half = two_ref.shape[0]
+    rest = jax.nn.gelu(dot(w2_ref[pl.ds(half, half), :], h_ref[...])).astype(BF16)
+    two = jnp.concatenate([two_ref[...], rest], axis=0)
     out_ref[...] = jax.nn.gelu(dot(w3_ref[...], two)).astype(BF16)
     token[...] = jnp.zeros(token.shape, F32)
 
 
-def chem_mid(hidden, layer_two, layer_three, table):
-    return pl.pallas_call(
-        chem_mid_kernel,
+def chem_layer(kernel, rows, table, *operands):
+    return pl.pallas_call(
+        kernel,
         out_shape=[
-            jax.ShapeDtypeStruct((layer_three.shape[0], hidden.shape[1]), BF16),
+            jax.ShapeDtypeStruct((rows, operands[0].shape[1]), BF16),
             token_shape(table),
         ],
-        in_specs=[VM] * 3,
+        in_specs=[VM] * len(operands),
         out_specs=[VM] * 2,
         compiler_params=GRANT,
-        cost_estimate=cost(2),
-        name="chem_mid",
-    )(hidden, layer_two, layer_three)
+        cost_estimate=cost(1),
+    )(*operands)
 
 
 def chem_out_kernel(h_ref, w4_ref, row_ref, hit_ref, out_ref, token):
@@ -473,9 +488,38 @@
                 scratch[pl.ds(((c + i) * 3 + k) * 8, 8), :] = jnp.where(at_wall, mirror, got)
 
 
-def flux_x_kernel(count, f_ref, r_ref, acc_ref, src_ref, *refs):
+def flux_x_inner_kernel(
+    f_ref, r_ref, acc_ref, src_ref, left, right, edge_ref, out_ref, token
+):
+    def line(c):
+        return [None] * 3 + [r_ref[rows8(c * 8 + x), :] for x in range(8)] + [None] * 3
+
+    face_states(line, left, right, 9, ((5, 8),))
+    flux = {f: face_flux(left, right, 9, 0, f) for f in (3, 4, 5)}
+    for c in range(COMPS):
+        edge_ref[pl.ds(c * 16, 8), :] = flux[3][c]
+        edge_ref[pl.ds(c * 16 + 8, 8), :] = flux[5][c]
+        for x in range(8):
+            at = pl.ds(c * 64 + x * 8, 8)
+            change = acc_ref[at, :]
+            if x in (3, 4):
+                change = change + (flux[x + 1][c] - flux[x][c])
+            new = f_ref[at, :] - TIME_STEP * change + CHEM_STEP * src_ref[at, :]
+            out_ref[c, pl.ds(x * 8, 8), :] = new
+    token[...] = jnp.zeros(token.shape, F32)
+
+
+def flux_x_kernel(count, r_ref, left_in, right_in, edge_ref, base_ref, *refs):
     flags = place_flags()
     layers, (out_hbm, lo_s, hi_s, left, right, out_ref, sems) = refs[:count], refs[count:]
+
+    def send(ref, first, planes):
+        rows = pl.ds(first * 8, planes * 8)
+        copy = pltpu.make_async_copy(ref.at[:, rows], out_hbm.at[:, rows], sems.at[first])
+        copy.start()
+        return copy
+
+    copies = [send(base_ref, 3, 2)]
 
     def own(c, x):
         return r_ref[pl.ds(c * 64 + x * 8, 8), :]
@@ -490,19 +534,29 @@
             + [hi_s[rows8(c * 3 + k), :] for k in range(3)]
         )
 
-    face_states(line, left, right, 9)
-    copies = []
-
-    def emit(c, x, change):
-        at, plane = pl.ds(c * 64 + x * 8, 8), pl.ds(x * 8, 8)
-        new = f_ref[at, :] - TIME_STEP * (acc_ref[at, :] + change) + CHEM_STEP * src_ref[at, :]
-        out_ref[c, plane, :] = new
-        if c == COMPS - 1:
-            here, there = out_ref.at[:, plane], out_hbm.at[:, plane]
-            copies.append(pltpu.make_async_copy(here, there, sems.at[x]))
-            copies[-1].start()
-
-    line_changes(left, right, 9, 0, emit)
+    face_states(line, left, right, 9, ((2, 4), (9, 11)))
+    for c in range(COMPS):
+        at = pl.ds((c * 9 + 2) * 8, 8)
+        right[at, :] = right_in[at, :]
+        at = pl.ds((c * 9 + 6) * 8, 8)
+        left[at, :] = left_in[at, :]
+
+    def emit(x, upper, lower):
+        plane = pl.ds(x * 8, 8)
+        for c in range(COMPS):
+            out_ref[c, plane, :] = base_ref[c, plane, :] - TIME_STEP * (upper[c] - lower[c])
+        copies.append(send(out_ref, x, 1))
+
+    flux = {
+        3: [edge_ref[pl.ds(c * 16, 8), :] for c in range(COMPS)],
+        5: [edge_ref[pl.ds(c * 16 + 8, 8), :] for c in range(COMPS)],
+    }
+    for f in (2, 1, 0):
+        flux[f] = face_flux(left, right, 9, 0, f)
+        emit(f, flux[f + 1], flux.pop(f) if f == 0 else flux[f])
+    for f in (6, 7, 8):
+        flux[f] = face_flux(left, right, 9, 0, f)
+        emit(f - 1, flux[f], flux[f - 1])
     for copy in copies:
         copy.wait()
 
@@ -608,11 +662,30 @@
     return jax.ShapeDtypeStruct(table.shape, F32)
 
 
-def flux_x(fields, recon, acc, source, layers):
+def flux_x_inner(fields, recon, acc, source, table):
+    states = jax.ShapeDtypeStruct((COMPS * 9 * 8, 128), F32)
+    return pl.pallas_call(
+        flux_x_inner_kernel,
+        out_shape=[
+            states,
+            states,
+            jax.ShapeDtypeStruct((COMPS * 16, 128), F32),
+            jax.ShapeDtypeStruct((COMPS, 64, 128), F32),
+            token_shape(table),
+        ],
+        in_specs=[VM] * 4,
+        out_specs=[VM] * 5,
+        compiler_params=GRANT,
+        cost_estimate=cost(1),
+        name="flux_x_inner",
+    )(fields, recon, acc, source)
+
+
+def flux_x(recon, inner, layers):
     return pl.pallas_call(
         lambda *a: flux_x_kernel(len(layers), *a),
         out_shape=jax.ShapeDtypeStruct((COMPS, 64, 128), F32),
-        in_specs=[VM] * (4 + len(layers)),
+        in_specs=[VM] * (5 + len(layers)),
         out_specs=HBM,
         scratch_shapes=halo_scratch()
         + state_scratch()
@@ -620,7 +693,7 @@
         compiler_params=GRANT,
         cost_estimate=cost(2),
         name="flux_x",
-    )(fields, recon, acc, source, *layers)
+    )(recon, *inner, *layers)
 
 
 def flux_y(recon, layers, table):
@@ -708,13 +781,16 @@
         y_got.append(swap_inner(y_second, "gy", "gz"))
     turned, *xs, z_first, z_second, token = turn(recon, pair_x, height)
     hidden, row_slot, hit, token_in = chem_in(recon, react, one, slots, table)
-    table = table + token + token_in
+    half, token_two = chem_layer(chem_two_kernel, layer_two.shape[0] // 2, table, hidden, two)
+    table = table + token + token_in + token_two
     if ride_y:
         table = table + join_table(y_got[0][layer_rows:], height)
     if not ride_z:
         table = sum_over(table, "gz")
     z_got = [swap(lax.dynamic_update_slice(z_first, table, (edge_rows, 0)), "gz", 0)]
-    hidden, token = chem_mid(hidden, two, three, table)
+    hidden, token = chem_layer(
+        chem_three_kernel, layer_three.shape[0], table, hidden, half, two, three
+    )
     if ride_z:
         table = table + z_got[0][edge_rows : edge_rows + height] + token
     if sizes[2] > 2:
@@ -729,7 +805,8 @@
     x_got = [swap(x, "gx", m) for m, x in enumerate(xs)]
     acc, token = flux_z(turned, acc, z_got, table)
     source, token_out = chem_out(hidden, four, row_slot, hit, table)
-    table = table + token + token_out
+    *inner, token_inner = flux_x_inner(flat, recon, acc, source, table)
+    table = table + token + token_out + token_inner
     if pair_x:
         table = table + join_table(x_got[0][layer_rows:], height)
     else:
@@ -739,9 +816,11 @@
         table = lax.psum(table, "gy")
     elif sizes[1] > 2:
         table = sum_over(table, "gy", 4)
-        pairs = [(i, i ^ 2) for i in range(sizes[1])]
-        rest = lax.ppermute(table, "gy", pairs)
-    new = flux_x(flat, recon, acc, source, x_got)
+        n, m = sizes[1], sizes[2]
+        flip = 1 - m % 2
+        pairs = [(i * m + j, (i ^ 2) * m + (j ^ flip)) for i in range(n) for j in range(m)]
+        rest = lax.ppermute(table, ("gy", "gz"), pairs)
+    new = flux_x(recon, inner, x_got)
     return new.reshape(shape), own_impulse(table, rest, own).reshape(own)
 
 

time: 24.7 us -> 23.9 us (0.968)
  the two profiles are of different devices: /device:TPU:0 before, /device:TPU:1 now
where the time goes in v1:
time: 23.9 us; the launch traced here: 23.8 us
  Pallas kernels  11.8 us (49%)
  starting transfers between devices  11 us (46%)
  between operations  0.75 us (3%)
    ppermute x4, starting transfers between devices, swap(): lax.ppermute(x, axis, [(a, b) for a, b in pairs] + [(b, a) for a, b in pa...  6.96 us
    ppermute x1, starting transfers between devices, body(): rest = lax.ppermute(table, ('gy', 'gz'), pairs)  3.98 us
    pallas_call x1, Pallas kernels, pack(): pl.pallas_call(pack_kernel, out_shape=outs, in_specs=[HBM] * 7, out_specs...  2.2 us
    pallas_call x2, Pallas kernels, chem_layer(): pl.pallas_call(kernel, out_shape=[jax.ShapeDtypeStruct((rows, operands[0]...  1.69 us
    pallas_call x1, Pallas kernels, flux_z(): pl.pallas_call(lambda *a: flux_z_kernel(len(layers), *a), out_shape=[jax....  1.61 us
    pallas_call x1, Pallas kernels, flux_x(): pl.pallas_call(lambda *a: flux_x_kernel(len(layers), *a), out_shape=jax.S...  1.5 us
    pallas_call x1, Pallas kernels, flux_y(): pl.pallas_call(lambda *a: flux_y_kernel(len(layers), *a), out_shape=[jax....  1.31 us
    pallas_call x1, Pallas kernels, chem_in(): pl.pallas_call(lambda *a: chem_in_kernel(slots, *a), out_shape=[jax.Shape...  1.24 us
  transfers between devices with their start and end apart: 6, of which 1 were waited for; matrix products, arithmetic and copies ran while one was open for 0% of the time, Pallas kernels for 38%

profile of v1, /device:TPU:1, one launch (start us, length us, event | category | flops | bytes accessed | tf_op | source)
XLA Modules:
  0.0 23.8 jit_solution(15256533786116801845)
XLA Ops:
  0.6 2.2 %pack.1 = (f32[768,128]{1,0:T(8,128)S(1)}, f32[768,128]{1,0:T(8,128)S(1)}, bf16[304,128]{1,0:T(8,128)(2,1)S(1)}, bf16[288,128]{1,0:T(8,128)(2,1)S(1)}, f32[2,128...) custom-call(f32[768,128]{1,0:T(8,128)} %bitcast.6, ...), custom_call_target="tpu_custom_call" | custom-call | bytes 7000000 | tf_op jit(solution)/shard_map/pack/pallas_call | solution.py:294
  2.8 2.2 %collective-permute-start = (bf16[304,128]{1,0:T(8,128)(2,1)S(1)}, bf16[304,128]{1,0:T(8,128)(2,1)S(1)}, u32[]{:S(2)}, u32[]{:S(2)}) collective-permute-start(bf16[304,128]{1,0:T(8,128)(2,1)S(1)} %get-tuple-element.39), channel_id=1, source_target_pairs={{0,4},{8,12},{4,0},{12,8},{1,5},{9,13},{5,1},{13,9},{2,6},{10,14},... | collective-permute-start | bytes 233480 | tf_op jit(solution)/shard_map/ppermute | solution.py:732
  5.0 0.3 %turn.1 = (f32[768,128]{1,0:T(8,128)S(1)}, bf16[304,128]{1,0:T(8,128)(2,1)S(1)}, f32[48,128]{1,0:T(8,128)S(1)}, f32[48,128]{1,0:T(8,128)S(1)}, f32[2,128]{1,0:T(2,128)S(1)}) custom-call(f32[768,128]{1,0:T(8,128)S(1)} %get-tuple-element.36.a_0_.r_ref), custom_call_target="tpu_custom_call" | custom-call | bytes 3500000 | tf_op jit(solution)/shard_map/turn/pallas_call | solution.py:342
  5.4 1.2 %chem_in.1 = (bf16[1600,128]{1,0:T(8,128)(2,1)S(1)}, bf16[64,128]{1,0:T(8,128)(2,1)S(1)}, bf16[128,128]{1,0:T(8,128)(2,1)S(1)}, f32[2,128]{1,0:T(2,128)S(1)}) custom-call(f32[768,128]{1,0:T(8,128)S(1)} %get-tuple-element.36.a_0_.r_ref, s32[64,128]{1,0:T(8,128)S(1)} %get-tuple-element.45.a_1_, bf16[12,1600]{1,0:T(8,128)(2,1)S(1)} %get-tuple-element.46.a_2_), custom_call_target="tpu_custom_call" | custom-call | bytes 3500000 | tf_op jit(solution)/shard_map/chem_in/pallas_call | solution.py:409
  6.6 0.6 %shard_map.86 = (bf16[400,128]{1,0:T(8,128)(2,1)S(1)}, f32[2,128]{1,0:T(2,128)S(1)}) custom-call(bf16[1600,128]{1,0:T(8,128)(2,1)S(1)} %get-tuple-element.48.h_ref, bf16[800,1600]{1,0:T(8,128)(2,1)S(1)} %get-tuple-element.49.w2_ref), custom_call_target="tpu_custom_call" | custom-call | bytes 3500000 | tf_op jit(solution)/shard_map/pallas_call | solution.py:440
  7.2 0.0 collective-permute-done.a_1_
  7.2 1.2 %collective-permute-start.2 = (f32[48,128]{1,0:T(8,128)S(1)}, f32[48,128]{1,0:T(8,128)S(1)}, u32[]{:S(2)}, u32[]{:S(2)}) collective-permute-start(f32[48,128]{1,0:T(8,128)S(1)} %get-tuple-element.70), channel_id=1, source_target_pairs={{0,1},{2,3},{1,0},{3,2},{4,5},{6,7},{5,4},{7,6},{8,9},{10,11},{9,8... | collective-permute-start | bytes 73736 | tf_op jit(solution)/shard_map/ppermute | solution.py:732
  8.4 0.1 collective-permute-start.1
  8.5 1.1 %shard_map.87 = (bf16[400,128]{1,0:T(8,128)(2,1)S(1)}, f32[2,128]{1,0:T(2,128)S(1)}) custom-call(bf16[1600,128]{1,0:T(8,128)(2,1)S(1)} %get-tuple-element.48.h_ref, bf16[400,128]{1,0:T(8,128)(2,1)S(1)} %get-tuple-element.52.two_ref, bf16[800,1600]{1,0:T(8,128)(2,1)S(1)} %get-tuple-element.49.w2_ref, bf16[400,800]{1,0:T(8,128)(2,1)S(1)} %get-tuple-element.53.w3_ref), custom_call_target="tpu_custom_call" | custom-call | bytes 3500000 | tf_op jit(solution)/shard_map/pallas_call | solution.py:440
  9.6 0.0 collective-permute-done.2.a_2_
  9.7 2.1 %collective-permute-start.3 = (f32[48,128]{1,0:T(8,128)S(1)}, f32[48,128]{1,0:T(8,128)S(1)}, u32[]{:S(2)}, u32[]{:S(2)}) collective-permute-start(f32[48,128]{1,0:T(8,128)S(1)} %constant_dynamic-update-slice_fusion), channel_id=1, source_target_pairs={{1,2},{0,3},{2,1},{3,0},{5,6},{4,7},{6,5},{7,4},{9,10},{8,11},{10,... | collective-permute-start | bytes 73736 | tf_op jit(solution)/shard_map/ppermute | solution.py:732
  11.7 0.0 collective-permute-done.1.a_2_
  11.7 1.3 %flux_y.1 = (f32[768,128]{1,0:T(8,128)S(1)}, f32[2,128]{1,0:T(2,128)S(1)}) custom-call(f32[768,128]{1,0:T(8,128)S(1)} %get-tuple-element.36.a_0_.r_ref, bf16[304,128]{1,0:T(8,128)(2,1)S(1)} %collective-permute-done.a_1_, bf16[288,128]{1,0:T(8,128)(2,1)S(1)} %collective-permute-done.1.a_2_), custom_call_target="tpu_custom_call" | custom-call | bytes 7000000 | tf_op jit(solution)/shard_map/flux_y/pallas_call | solution.py:700
  13.1 0.2 collective-permute-done.3.a_3_
  13.3 1.5 %collective-permute-start.4 = (bf16[304,128]{1,0:T(8,128)(2,1)S(1)}, bf16[304,128]{1,0:T(8,128)(2,1)S(1)}, u32[]{:S(2)}, u32[]{:S(2)}) collective-permute-start(bf16[304,128]{1,0:T(8,128)(2,1)S(1)} %put_table.1), channel_id=1, source_target_pairs={{0,16},{16,0},{1,17},{17,1},{2,18},{18,2},{3,19},{19,3},{4,20},{20... | collective-permute-start | bytes 233480 | tf_op jit(solution)/shard_map/ppermute | solution.py:732
  14.8 0.7 %chem_out.1 = (f32[768,128]{1,0:T(8,128)S(1)}, f32[2,128]{1,0:T(2,128)S(1)}) custom-call(bf16[400,128]{1,0:T(8,128)(2,1)S(1)} %get-tuple-element.56.h_ref, bf16[12,400]{1,0:T(8,128)(2,1)S(1)} %get-tuple-element.57.w4_ref, bf16[64,128]{1,0:T(8,128)(2,1)S(1)} %get-tuple-element.58.row_ref, bf16[128,128]{1,0:T(8,128)(2,1)S(1)} %get-tuple-element.59.hit_ref), custom_call_target="tpu_custom_call" | custom-call | bytes 3500000 | tf_op jit(solution)/shard_map/chem_out/pallas_call | solution.py:466
  15.4 1.6 %flux_z.1 = (f32[768,128]{1,0:T(8,128)S(1)}, f32[2,128]{1,0:T(2,128)S(1)}) custom-call(f32[768,128]{1,0:T(8,128)S(1)} %get-tuple-element.38.a_0_, f32[768,128]{1,0:T(8,128)S(1)} %get-tuple-element.41.a_1_, f32[48,128]{1,0:T(8,128)S(1)} %collective-permute-done.2.a_2_, f32[48,128]{1,0:T(8,128)S(1)} %collective-permute-done.3.a_3_), custom_call_target="tpu_custom_call" | custom-call | bytes 7000000 | tf_op jit(solution)/shard_map/flux_z/pallas_call | solution.py:713
  17.0 0.6 %flux_x_inner.1 = (f32[864,128]{1,0:T(8,128)S(1)}, f32[864,128]{1,0:T(8,128)S(1)}, f32[192,128]{1,0:T(8,128)S(1)}, f32[12,64,128]{2,1,0:T(8,128)S(1)}, f32[2,128]{1,0:T(2,128)S(1)}) custom-call(f32[768,128]{1,0:T(8,128)S(1)} %get-tuple-element.37.f_ref, f32[768,128]{1,0:T(8,128)S(1)} %get-tuple-element.36.a_0_.r_ref, ...), custom_call_target="tpu_custom_call" | custom-call | bytes 3500000 | tf_op jit(solution)/shard_map/flux_x_inner/pallas_call | solution.py:667
  17.6 0.0 collective-permute-done.4.a_5_
  17.7 4.0 %collective-permute-start.5 = (f32[2,128]{1,0:T(2,128)S(1)}, f32[2,128]{1,0:T(2,128)S(1)}, u32[]{:S(2)}, u32[]{:S(2)}) collective-permute-start(f32[2,128]{1,0:T(2,128)S(1)} %add_add_fusion.a_0_), channel_id=1, source_target_pairs={{0,9},{1,8},{2,11},{3,10},{4,13},{5,12},{6,15},{7,14},{8,1},{9,0},... | collective-permute-start | bytes 3080 | tf_op jit(solution)/shard_map/ppermute | solution.py:822
  21.7 1.5 %flux_x.1 = f32[12,64,128]{2,1,0:T(8,128)} custom-call(f32[768,128]{1,0:T(8,128)S(1)} %get-tuple-element.36.a_0_.r_ref, f32[864,128]{1,0:T(8,128)S(1)} %get-tuple-element.61.a_1_, f32[864,128]{1,0:T(8,128)S(1)} %get-tuple-element.62.a_2_, f32[192,128]{1,0:T(8,128)S(1)} %get-tuple-element.63.a_3_, f32[12,64,128]{2,1,0:T(8,128)S(1)} %get-tuple-element.64.a_4_, ...), custom_call_target="tpu_custom_call" | custom-call | bytes 7000000 | tf_op jit(solution)/shard_map/flux_x/pallas_call | solution.py:685
  23.2 0.0 collective-permute-done.5.a_1_
  23.2 0.6 %impulse.1 = f32[1,8]{1,0:T(1,128)} custom-call(f32[2,128]{1,0:T(2,128)S(1)} %add_add_fusion.a_0_, f32[2,128]{1,0:T(2,128)S(1)} %collective-permute-done.5.a_1_), custom_call_target="tpu_custom_call" | custom-call | bytes 1750000 | tf_op jit(solution)/shard_map/impulse/pallas_call | solution.py:642
  (7 shorter events, 0.1 us)
Async XLA Ops:
  2.8 4.3 %collective-permute-start = (bf16[304,128]{1,0:T(8,128)(2,1)S(1)}, bf16[304,128]{1,0:T(8,128)(2,1)S(1)}, u32[]{:S(2)}, u32[]{:S(2)}) collective-permute-start(bf16[304,128]{1,0:T(8,128)(2,1)S(1)} %get-tuple-element.39), channel_id=1, source_target_pairs={{0,4},{8,12},{4,0},{12,8},{1,5},{9,13},{5,1},{13,9},{2,6},{10,14},... | collective-permute-start | bytes 233480 | tf_op jit(solution)/shard_map/ppermute | solution.py:732
  7.2 2.4 %collective-permute-start.2 = (f32[48,128]{1,0:T(8,128)S(1)}, f32[48,128]{1,0:T(8,128)S(1)}, u32[]{:S(2)}, u32[]{:S(2)}) collective-permute-start(f32[48,128]{1,0:T(8,128)S(1)} %get-tuple-element.70), channel_id=1, source_target_pairs={{0,1},{2,3},{1,0},{3,2},{4,5},{6,7},{5,4},{7,6},{8,9},{10,11},{9,8... | collective-permute-start | bytes 73736 | tf_op jit(solution)/shard_map/ppermute | solution.py:732
  8.4 3.3 %collective-permute-start.1 = (bf16[288,128]{1,0:T(8,128)(2,1)S(1)}, bf16[288,128]{1,0:T(8,128)(2,1)S(1)}, u32[]{:S(2)}, u32[]{:S(2)}) collective-permute-start(bf16[288,128]{1,0:T(8,128)(2,1)S(1)} %get-tuple-element.40), channel_id=1, source_target_pairs={{0,1},{1,0},{2,3},{3,2},{4,8},{5,9},{6,10},{7,11},{8,4},{9,5},{10,... | collective-permute-start | bytes 221192 | tf_op jit(solution)/shard_map/ppermute | solution.py:745
  9.7 3.6 %collective-permute-start.3 = (f32[48,128]{1,0:T(8,128)S(1)}, f32[48,128]{1,0:T(8,128)S(1)}, u32[]{:S(2)}, u32[]{:S(2)}) collective-permute-start(f32[48,128]{1,0:T(8,128)S(1)} %constant_dynamic-update-slice_fusion), channel_id=1, source_target_pairs={{1,2},{0,3},{2,1},{3,0},{5,6},{4,7},{6,5},{7,4},{9,10},{8,11},{10,... | collective-permute-start | bytes 73736 | tf_op jit(solution)/shard_map/ppermute | solution.py:732
  13.3 4.4 %collective-permute-start.4 = (bf16[304,128]{1,0:T(8,128)(2,1)S(1)}, bf16[304,128]{1,0:T(8,128)(2,1)S(1)}, u32[]{:S(2)}, u32[]{:S(2)}) collective-permute-start(bf16[304,128]{1,0:T(8,128)(2,1)S(1)} %put_table.1), channel_id=1, source_target_pairs={{0,16},{16,0},{1,17},{17,1},{2,18},{18,2},{3,19},{19,3},{4,20},{20... | collective-permute-start | bytes 233480 | tf_op jit(solution)/shard_map/ppermute | solution.py:732
  17.7 5.5 %collective-permute-start.5 = (f32[2,128]{1,0:T(2,128)S(1)}, f32[2,128]{1,0:T(2,128)S(1)}, u32[]{:S(2)}, u32[]{:S(2)}) collective-permute-start(f32[2,128]{1,0:T(2,128)S(1)} %add_add_fusion.a_0_), channel_id=1, source_target_pairs={{0,9},{1,8},{2,11},{3,10},{4,13},{5,12},{6,15},{7,14},{8,1},{9,0},... | collective-permute-start | bytes 3080 | tf_op jit(solution)/shard_map/ppermute | solution.py:822

commit v2 on v1

--- a/solution.py
+++ b/solution.py
@@ -168,11 +168,11 @@
 
 
 def pack_kernel(*refs):
-    f_hbm, map_hbm, *sources = refs[:7]
-    f_ref, r_ref, y1_ref, y2_ref, table_ref, *kept = refs[7:17]
-    buf, map_ref, sems = refs[17:]
+    f_hbm, map_hbm, *sources = refs[:5]
+    f_ref, r_ref, y1_ref, y2_ref, table_ref, *kept = refs[5:13]
+    buf, map_ref, sems = refs[13:]
     pairs = [(f_hbm, f_ref, 8), (map_hbm, map_ref, 1)]
-    pairs += list(zip(sources, kept, (1, 1, 8, 4, 1)))
+    pairs += list(zip(sources, kept, (1, 1, 1)))
     waits = [fetch(a, b, sems.at[i], parts) for i, (a, b, parts) in enumerate(pairs)]
     flags = place_flags()
     waits[0]()
@@ -288,23 +288,23 @@
     outs.append(jax.ShapeDtypeStruct((COMPS * 24 + load_rows(height), 128), BF16))
     outs.append(jax.ShapeDtypeStruct((COMPS * 24, 128), BF16))
     outs.append(jax.ShapeDtypeStruct((height, 128), F32))
-    one, two, three, four = layers
-    kept = [jax.ShapeDtypeStruct(x.shape, x.dtype) for x in (react, one, two, three, four)]
+    one, _, _, four = layers
+    kept = [jax.ShapeDtypeStruct(x.shape, x.dtype) for x in (react, one, four)]
     outs += kept
     return pl.pallas_call(
         pack_kernel,
         out_shape=outs,
-        in_specs=[HBM] * 7,
+        in_specs=[HBM] * 5,
         out_specs=[VM] * len(outs),
         scratch_shapes=[
             pltpu.VMEM((128, 128), F32),
             pltpu.VMEM(panels.shape, jnp.int32),
-            pltpu.SemaphoreType.DMA((7,)),
+            pltpu.SemaphoreType.DMA((5,)),
         ],
         compiler_params=GRANT,
         cost_estimate=cost(2),
         name="pack",
-    )(*map(in_hbm, (fields, panels, react, *layers)))
+    )(*map(in_hbm, (fields, panels, react, one, four)))
 
 
 def turn_kernel(pair_x, r_ref, zt_ref, *refs):
@@ -351,7 +351,7 @@
 
 
 def cost(us):
-    return pl.CostEstimate(flops=0, transcendentals=0, bytes_accessed=int(us * 3.5e6))
+    return pl.CostEstimate(flops=int(0.6*us*1e9), transcendentals=0, bytes_accessed=int(us * 0.6*3.5e6))
 
 
 def dot(a, b):
@@ -428,7 +428,7 @@
     token[...] = jnp.zeros(token.shape, F32)
 
 
-def chem_three_kernel(h_ref, two_ref, w2_ref, w3_ref, out_ref, token):
+def chem_three_kernel(h_ref, two_ref, w2_ref, w3_ref, _, out_ref, token):
     half = two_ref.shape[0]
     rest = jax.nn.gelu(dot(w2_ref[pl.ds(half, half), :], h_ref[...])).astype(BF16)
     two = jnp.concatenate([two_ref[...], rest], axis=0)
@@ -450,7 +450,7 @@
     )(*operands)
 
 
-def chem_out_kernel(h_ref, w4_ref, row_ref, hit_ref, out_ref, token):
+def chem_out_kernel(h_ref, w4_ref, row_ref, hit_ref, _, out_ref, token):
     rates = dot(w4_ref[...], h_ref[...])
     slots = rates.shape[1]
     rates = jnp.concatenate([rates, jnp.zeros((128 - COMPS, slots), F32)], axis=0)
@@ -466,12 +466,12 @@
     return pl.pallas_call(
         chem_out_kernel,
         out_shape=[jax.ShapeDtypeStruct((COMPS * 64, 128), F32), token_shape(table)],
-        in_specs=[VM] * 4,
+        in_specs=[VM] * 5,
         out_specs=[VM] * 2,
         compiler_params=GRANT,
         cost_estimate=cost(1),
         name="chem_out",
-    )(hidden, layer_four, row_slot, hit)
+    )(hidden, layer_four, row_slot, hit, table)
 
 
 def halo_lines(refs, scratch, own, sign_comp, at_wall, order, second):
@@ -775,7 +775,8 @@
     panels, react = panel_map.reshape(-1, shape[3]), reacting.reshape(-1, shape[3])
     layers = (layer_one.T, layer_two, layer_three, layer_four)
     packed = pack(flat, panels, react, layers, height)
-    flat, recon, y_first, y_second, table, react, one, two, three, four = packed
+    flat, recon, y_first, y_second, table, react, one, four = packed
+    two, three = layer_two, layer_three
     y_got = [swap(y_first, "gy", 0)]
     if sizes[1] > 2:
         y_got.append(swap_inner(y_second, "gy", "gz"))
@@ -789,7 +790,7 @@
         table = sum_over(table, "gz")
     z_got = [swap(lax.dynamic_update_slice(z_first, table, (edge_rows, 0)), "gz", 0)]
     hidden, token = chem_layer(
-        chem_three_kernel, layer_three.shape[0], table, hidden, half, two, three
+        chem_three_kernel, layer_three.shape[0], table, hidden, half, two, three, table
     )
     if ride_z:
         table = table + z_got[0][edge_rows : edge_rows + height] + token

time: 23.9 us -> 22.2 us (0.929)
  the two profiles are of different devices: /device:TPU:1 before, /device:TPU:0 now
where the time goes in v2:
time: 22.2 us; the launch traced here: 21.9 us
  Pallas kernels  11.1 us (50%)
  starting transfers between devices  9.34 us (42%)
  between operations  0.73 us (3%)
  waiting for transfers between devices  0.65 us (3%)
    ppermute x4, starting transfers between devices, swap(): lax.ppermute(x, axis, [(a, b) for a, b in pairs] + [(b, a) for a, b in pa...  6.99 us
    ppermute x1, starting transfers between devices, body(): rest = lax.ppermute(table, ('gy', 'gz'), pairs)  2.35 us
    pallas_call x2, Pallas kernels, chem_layer(): pl.pallas_call(kernel, out_shape=[jax.ShapeDtypeStruct((rows, operands[0]...  1.67 us
    pallas_call x1, Pallas kernels, flux_z(): pl.pallas_call(lambda *a: flux_z_kernel(len(layers), *a), out_shape=[jax....  1.61 us
    pallas_call x1, Pallas kernels, pack(): pl.pallas_call(pack_kernel, out_shape=outs, in_specs=[HBM] * 5, out_specs...  1.59 us
    pallas_call x1, Pallas kernels, flux_x(): pl.pallas_call(lambda *a: flux_x_kernel(len(layers), *a), out_shape=jax.S...  1.5 us
    pallas_call x1, Pallas kernels, flux_y(): pl.pallas_call(lambda *a: flux_y_kernel(len(layers), *a), out_shape=[jax....  1.31 us
    pallas_call x1, Pallas kernels, chem_in(): pl.pallas_call(lambda *a: chem_in_kernel(slots, *a), out_shape=[jax.Shape...  1.24 us
  transfers between devices with their start and end apart: 6, of which 4 were waited for; matrix products, arithmetic and copies ran while one was open for 0% of the time, Pallas kernels for 41%

profile of v2, /device:TPU:0, one launch (start us, length us, event | category | flops | bytes accessed | tf_op | source)
XLA Modules:
  0.0 21.9 jit_solution(10311006399488474194)
XLA Ops:
  0.6 1.6 %pack.1 = (f32[768,128]{1,0:T(8,128)S(1)}, f32[768,128]{1,0:T(8,128)S(1)}, bf16[304,128]{1,0:T(8,128)(2,1)S(1)}, bf16[288,128]{1,0:T(8,128)(2,1)S(1)}, f32[2,128...) custom-call(f32[768,128]{1,0:T(8,128)} %bitcast.6, ...), custom_call_target="tpu_custom_call" | custom-call | flops 1200000000 | bytes 4200000 | tf_op jit(solution)/shard_map/pack/pallas_call | solution.py:294
  2.2 0.0 copy-start
  2.2 3.1 %collective-permute-start = (bf16[304,128]{1,0:T(8,128)(2,1)S(1)}, bf16[304,128]{1,0:T(8,128)(2,1)S(1)}, u32[]{:S(2)}, u32[]{:S(2)}) collective-permute-start(bf16[304,128]{1,0:T(8,128)(2,1)S(1)} %get-tuple-element.37), channel_id=1, source_target_pairs={{0,4},{8,12},{4,0},{12,8},{1,5},{9,13},{5,1},{13,9},{2,6},{10,14},... | collective-permute-start | bytes 233480 | tf_op jit(solution)/shard_map/ppermute | solution.py:732
  5.4 0.0 collective-permute-start.1
  5.4 0.3 %turn.1 = (f32[768,128]{1,0:T(8,128)S(1)}, bf16[304,128]{1,0:T(8,128)(2,1)S(1)}, f32[48,128]{1,0:T(8,128)S(1)}, f32[48,128]{1,0:T(8,128)S(1)}, f32[2,128]{1,0:T(2,128)S(1)}) custom-call(f32[768,128]{1,0:T(8,128)S(1)} %get-tuple-element.34.a_0_.r_ref), custom_call_target="tpu_custom_call" | custom-call | flops 600000000 | bytes 2100000 | tf_op jit(solution)/shard_map/turn/pallas_call | solution.py:342
  5.7 0.0 copy-start.1
  5.7 1.2 %chem_in.1 = (bf16[1600,128]{1,0:T(8,128)(2,1)S(1)}, bf16[64,128]{1,0:T(8,128)(2,1)S(1)}, bf16[128,128]{1,0:T(8,128)(2,1)S(1)}, f32[2,128]{1,0:T(2,128)S(1)}) custom-call(f32[768,128]{1,0:T(8,128)S(1)} %get-tuple-element.34.a_0_.r_ref, s32[64,128]{1,0:T(8,128)S(1)} %get-tuple-element.43.a_1_, bf16[12,1600]{1,0:T(8,128)(2,1)S(1)} %get-tuple-element.44.a_2_), custom_call_target="tpu_custom_call" | custom-call | flops 600000000 | bytes 2100000 | tf_op jit(solution)/shard_map/chem_in/pallas_call | solution.py:409
  7.0 0.6 %shard_map.86 = (bf16[400,128]{1,0:T(8,128)(2,1)S(1)}, f32[2,128]{1,0:T(2,128)S(1)}) custom-call(bf16[1600,128]{1,0:T(8,128)(2,1)S(1)} %get-tuple-element.46.h_ref, bf16[800,1600]{1,0:T(8,128)(2,1)S(1)} %copy-done), custom_call_target="tpu_custom_call" | custom-call | flops 600000000 | bytes 2100000 | tf_op jit(solution)/shard_map/pallas_call | solution.py:440
  7.5 0.2 collective-permute-done.a_1_
  7.8 0.4 %collective-permute-start.2 = (f32[48,128]{1,0:T(8,128)S(1)}, f32[48,128]{1,0:T(8,128)S(1)}, u32[]{:S(2)}, u32[]{:S(2)}) collective-permute-start(f32[48,128]{1,0:T(8,128)S(1)} %get-tuple-element.66), channel_id=1, source_target_pairs={{0,1},{2,3},{1,0},{3,2},{4,5},{6,7},{5,4},{7,6},{8,9},{10,11},{9,8... | collective-permute-start | bytes 73736 | tf_op jit(solution)/shard_map/ppermute | solution.py:732
  8.1 1.1 %shard_map.87 = (bf16[400,128]{1,0:T(8,128)(2,1)S(1)}, f32[2,128]{1,0:T(2,128)S(1)}) custom-call(bf16[1600,128]{1,0:T(8,128)(2,1)S(1)} %get-tuple-element.46.h_ref, bf16[400,128]{1,0:T(8,128)(2,1)S(1)} %get-tuple-element.49.two_ref, bf16[800,1600]{1,0:T(8,128)(2,1)S(1)} %copy-done, bf16[400,800]{1,0:T(8,128)(2,1)S(1)} %copy-done.1, ...), custom_call_target="tpu_custom_call" | custom-call | flops 600000000 | bytes 2100000 | tf_op jit(solution)/shard_map/pallas_call | solution.py:440
  9.3 0.0 collective-permute-done.2.a_2_
  9.3 1.8 %collective-permute-start.3 = (f32[48,128]{1,0:T(8,128)S(1)}, f32[48,128]{1,0:T(8,128)S(1)}, u32[]{:S(2)}, u32[]{:S(2)}) collective-permute-start(f32[48,128]{1,0:T(8,128)S(1)} %constant_dynamic-update-slice_fusion), channel_id=1, source_target_pairs={{1,2},{0,3},{2,1},{3,0},{5,6},{4,7},{6,5},{7,4},{9,10},{8,11},{10,... | collective-permute-start | bytes 73736 | tf_op jit(solution)/shard_map/ppermute | solution.py:732
  11.1 1.3 %flux_y.1 = (f32[768,128]{1,0:T(8,128)S(1)}, f32[2,128]{1,0:T(2,128)S(1)}) custom-call(f32[768,128]{1,0:T(8,128)S(1)} %get-tuple-element.34.a_0_.r_ref, bf16[304,128]{1,0:T(8,128)(2,1)S(1)} %collective-permute-done.a_1_, bf16[288,128]{1,0:T(8,128)(2,1)S(1)} %collective-permute-done.1.a_2_), custom_call_target="tpu_custom_call" | custom-call | flops 1200000000 | bytes 4200000 | tf_op jit(solution)/shard_map/flux_y/pallas_call | solution.py:700
  12.4 0.2 collective-permute-done.3.a_3_
  12.7 1.7 %collective-permute-start.4 = (bf16[304,128]{1,0:T(8,128)(2,1)S(1)}, bf16[304,128]{1,0:T(8,128)(2,1)S(1)}, u32[]{:S(2)}, u32[]{:S(2)}) collective-permute-start(bf16[304,128]{1,0:T(8,128)(2,1)S(1)} %put_table.1), channel_id=1, source_target_pairs={{0,16},{16,0},{1,17},{17,1},{2,18},{18,2},{3,19},{19,3},{4,20},{20... | collective-permute-start | bytes 233480 | tf_op jit(solution)/shard_map/ppermute | solution.py:732
  14.3 1.6 %flux_z.1 = (f32[768,128]{1,0:T(8,128)S(1)}, f32[2,128]{1,0:T(2,128)S(1)}) custom-call(f32[768,128]{1,0:T(8,128)S(1)} %get-tuple-element.36.a_0_, f32[768,128]{1,0:T(8,128)S(1)} %get-tuple-element.39.a_1_, f32[48,128]{1,0:T(8,128)S(1)} %collective-permute-done.2.a_2_, f32[48,128]{1,0:T(8,128)S(1)} %collective-permute-done.3.a_3_), custom_call_target="tpu_custom_call" | custom-call | flops 1200000000 | bytes 4200000 | tf_op jit(solution)/shard_map/flux_z/pallas_call | solution.py:713
  15.9 0.7 %chem_out.1 = (f32[768,128]{1,0:T(8,128)S(1)}, f32[2,128]{1,0:T(2,128)S(1)}) custom-call(bf16[400,128]{1,0:T(8,128)(2,1)S(1)} %get-tuple-element.52.h_ref, bf16[12,400]{1,0:T(8,128)(2,1)S(1)} %get-tuple-element.53.w4_ref, bf16[64,128]{1,0:T(8,128)(2,1)S(1)} %get-tuple-element.54.row_ref, bf16[128,128]{1,0:T(8,128)(2,1)S(1)} %get-tuple-element.55.hit_ref, ...), custom_call_target="tpu_custom_call" | custom-call | flops 600000000 | bytes 2100000 | tf_op jit(solution)/shard_map/chem_out/pallas_call | solution.py:466
  16.6 0.6 %flux_x_inner.1 = (f32[864,128]{1,0:T(8,128)S(1)}, f32[864,128]{1,0:T(8,128)S(1)}, f32[192,128]{1,0:T(8,128)S(1)}, f32[12,64,128]{2,1,0:T(8,128)S(1)}, f32[2,128]{1,0:T(2,128)S(1)}) custom-call(f32[768,128]{1,0:T(8,128)S(1)} %get-tuple-element.35.f_ref, f32[768,128]{1,0:T(8,128)S(1)} %get-tuple-element.34.a_0_.r_ref, ...), custom_call_target="tpu_custom_call" | custom-call | flops 600000000 | bytes 2100000 | tf_op jit(solution)/shard_map/flux_x_inner/pallas_call | solution.py:667
  17.2 0.1 collective-permute-done.4.a_5_
  17.3 2.4 %collective-permute-start.5 = (f32[2,128]{1,0:T(2,128)S(1)}, f32[2,128]{1,0:T(2,128)S(1)}, u32[]{:S(2)}, u32[]{:S(2)}) collective-permute-start(f32[2,128]{1,0:T(2,128)S(1)} %add_add_fusion.a_0_), channel_id=1, source_target_pairs={{0,9},{1,8},{2,11},{3,10},{4,13},{5,12},{6,15},{7,14},{8,1},{9,0},... | collective-permute-start | bytes 3080 | tf_op jit(solution)/shard_map/ppermute | solution.py:823
  19.7 1.5 %flux_x.1 = f32[12,64,128]{2,1,0:T(8,128)} custom-call(f32[768,128]{1,0:T(8,128)S(1)} %get-tuple-element.34.a_0_.r_ref, f32[864,128]{1,0:T(8,128)S(1)} %get-tuple-element.58.a_1_, f32[864,128]{1,0:T(8,128)S(1)} %get-tuple-element.59.a_2_, f32[192,128]{1,0:T(8,128)S(1)} %get-tuple-element.60.a_3_, f32[12,64,128]{2,1,0:T(8,128)S(1)} %get-tuple-element.61.a_4_, ...), custom_call_target="tpu_custom_call" | custom-call | flops 1200000000 | bytes 4200000 | tf_op jit(solution)/shard_map/flux_x/pallas_call | solution.py:685
  21.2 0.1 collective-permute-done.5.a_1_
  21.3 0.6 %impulse.1 = f32[1,8]{1,0:T(1,128)} custom-call(f32[2,128]{1,0:T(2,128)S(1)} %add_add_fusion.a_0_, f32[2,128]{1,0:T(2,128)S(1)} %collective-permute-done.5.a_1_), custom_call_target="tpu_custom_call" | custom-call | flops 300000000 | bytes 1050000 | tf_op jit(solution)/shard_map/impulse/pallas_call | solution.py:642
  (10 shorter events, 0.1 us)
Async XLA Ops:
  2.2 4.7 %copy-start = (bf16[800,1600]{1,0:T(8,128)(2,1)S(1)}, bf16[800,1600]{1,0:T(8,128)(2,1)}, u32[]{:S(2)}) copy-start(bf16[800,1600]{1,0:T(8,128)(2,1)} %w2_ref.3) | copy-start | bytes 7680004
  2.2 5.5 %collective-permute-start = (bf16[304,128]{1,0:T(8,128)(2,1)S(1)}, bf16[304,128]{1,0:T(8,128)(2,1)S(1)}, u32[]{:S(2)}, u32[]{:S(2)}) collective-permute-start(bf16[304,128]{1,0:T(8,128)(2,1)S(1)} %get-tuple-element.37), channel_id=1, source_target_pairs={{0,4},{8,12},{4,0},{12,8},{1,5},{9,13},{5,1},{13,9},{2,6},{10,14},... | collective-permute-start | bytes 233480 | tf_op jit(solution)/shard_map/ppermute | solution.py:732
  5.4 5.8 %collective-permute-start.1 = (bf16[288,128]{1,0:T(8,128)(2,1)S(1)}, bf16[288,128]{1,0:T(8,128)(2,1)S(1)}, u32[]{:S(2)}, u32[]{:S(2)}) collective-permute-start(bf16[288,128]{1,0:T(8,128)(2,1)S(1)} %get-tuple-element.38), channel_id=1, source_target_pairs={{0,1},{1,0},{2,3},{3,2},{4,8},{5,9},{6,10},{7,11},{8,4},{9,5},{10,... | collective-permute-start | bytes 221192 | tf_op jit(solution)/shard_map/ppermute | solution.py:745
  5.7 2.4 %copy-start.1 = (bf16[400,800]{1,0:T(8,128)(2,1)S(1)}, bf16[400,800]{1,0:T(8,128)(2,1)}, u32[]{:S(2)}) copy-start(bf16[400,800]{1,0:T(8,128)(2,1)} %w3_ref.1) | copy-start | bytes 1920004
  7.8 1.5 %collective-permute-start.2 = (f32[48,128]{1,0:T(8,128)S(1)}, f32[48,128]{1,0:T(8,128)S(1)}, u32[]{:S(2)}, u32[]{:S(2)}) collective-permute-start(f32[48,128]{1,0:T(8,128)S(1)} %get-tuple-element.66), channel_id=1, source_target_pairs={{0,1},{2,3},{1,0},{3,2},{4,5},{6,7},{5,4},{7,6},{8,9},{10,11},{9,8... | collective-permute-start | bytes 73736 | tf_op jit(solution)/shard_map/ppermute | solution.py:732
  9.3 3.3 %collective-permute-start.3 = (f32[48,128]{1,0:T(8,128)S(1)}, f32[48,128]{1,0:T(8,128)S(1)}, u32[]{:S(2)}, u32[]{:S(2)}) collective-permute-start(f32[48,128]{1,0:T(8,128)S(1)} %constant_dynamic-update-slice_fusion), channel_id=1, source_target_pairs={{1,2},{0,3},{2,1},{3,0},{5,6},{4,7},{6,5},{7,4},{9,10},{8,11},{10,... | collective-permute-start | bytes 73736 | tf_op jit(solution)/shard_map/ppermute | solution.py:732
  12.7 4.7 %collective-permute-start.4 = (bf16[304,128]{1,0:T(8,128)(2,1)S(1)}, bf16[304,128]{1,0:T(8,128)(2,1)S(1)}, u32[]{:S(2)}, u32[]{:S(2)}) collective-permute-start(bf16[304,128]{1,0:T(8,128)(2,1)S(1)} %put_table.1), channel_id=1, source_target_pairs={{0,16},{16,0},{1,17},{17,1},{2,18},{18,2},{3,19},{19,3},{4,20},{20... | collective-permute-start | bytes 233480 | tf_op jit(solution)/shard_map/ppermute | solution.py:732
  17.3 4.0 %collective-permute-start.5 = (f32[2,128]{1,0:T(2,128)S(1)}, f32[2,128]{1,0:T(2,128)S(1)}, u32[]{:S(2)}, u32[]{:S(2)}) collective-permute-start(f32[2,128]{1,0:T(2,128)S(1)} %add_add_fusion.a_0_), channel_id=1, source_target_pairs={{0,9},{1,8},{2,11},{3,10},{4,13},{5,12},{6,15},{7,14},{8,1},{9,0},... | collective-permute-start | bytes 3080 | tf_op jit(solution)/shard_map/ppermute | solution.py:823

commit v3 on v2

--- a/solution.py
+++ b/solution.py
@@ -169,8 +169,8 @@
 
 def pack_kernel(*refs):
     f_hbm, map_hbm, *sources = refs[:5]
-    f_ref, r_ref, y1_ref, y2_ref, table_ref, *kept = refs[5:13]
-    buf, map_ref, sems = refs[13:]
+    f_ref, r_ref, y1_ref, table_ref, *kept = refs[5:12]
+    buf, map_ref, sems = refs[12:]
     pairs = [(f_hbm, f_ref, 8), (map_hbm, map_ref, 1)]
     pairs += list(zip(sources, kept, (1, 1, 1)))
     waits = [fetch(a, b, sems.at[i], parts) for i, (a, b, parts) in enumerate(pairs)]
@@ -230,13 +230,7 @@
             total = total + jnp.where(panel == lane + 128.0 * j, load, 0.0)
         table.append(jnp.sum(total, axis=0, keepdims=True))
         table_ref[pl.ds(j, 1), :] = table[j]
-    for c in range(0, COMPS, 2):
-        def row(i, y):
-            return r_ref[pl.ds((c + i) * 64 + y, 8, stride=8), :]
-
-        lo = jnp.concatenate([row(i, y) for i in (0, 1) for y in range(3)], axis=0)
-        hi = jnp.concatenate([row(i, y) for i in (0, 1) for y in range(5, 8)], axis=0)
-        store_layers((y1_ref, y2_ref), c, lo, hi, flags[7])
+    store_y_layers(r_ref, y1_ref, flags[7] == 0)
     rows = y1_ref.shape[0] - COMPS * 24
     pieces = [piece[j] for piece in zip(*map(split3, table)) for j in range(len(table))]
     if rows > len(pieces):
@@ -244,6 +238,16 @@
     y1_ref[pl.ds(COMPS * 24, rows), :] = jnp.concatenate(pieces, axis=0).astype(BF16)
     for wait in waits[2:]:
         wait()
+
+
+def store_y_layers(r_ref, ref, upper):
+    for c in range(0, COMPS, 2):
+        def row(i, y):
+            return r_ref[pl.ds((c + i) * 64 + y, 8, stride=8), :]
+
+        lo = jnp.concatenate([row(i, y) for i in (0, 1) for y in range(3)], axis=0)
+        hi = jnp.concatenate([row(i, y) for i in (0, 1) for y in range(5, 8)], axis=0)
+        ref[pl.ds(c * 24, 48), :] = jnp.where(upper, hi, lo).astype(BF16)
 
 
 def store_layers(refs, c, lo, hi, parity):
@@ -286,7 +290,6 @@
     whole = jax.ShapeDtypeStruct((COMPS * 64, 128), F32)
     outs = [whole, whole]
     outs.append(jax.ShapeDtypeStruct((COMPS * 24 + load_rows(height), 128), BF16))
-    outs.append(jax.ShapeDtypeStruct((COMPS * 24, 128), BF16))
     outs.append(jax.ShapeDtypeStruct((height, 128), F32))
     one, _, _, four = layers
     kept = [jax.ShapeDtypeStruct(x.shape, x.dtype) for x in (react, one, four)]
@@ -351,13 +354,19 @@
 
 
 def cost(us):
-    return pl.CostEstimate(flops=int(0.6*us*1e9), transcendentals=0, bytes_accessed=int(us * 0.6*3.5e6))
+    return pl.CostEstimate(flops=int(us * 0.8e9), transcendentals=0, bytes_accessed=int(us * 2.8e6))
 
 
 def dot(a, b):
     return jnp.dot(a, b, preferred_element_type=F32)
 
 
+def gelu(x):
+    half = 0.5 * x
+    root = (2.0 / 3.141592653589793) ** 0.5
+    return half + half * jnp.tanh(x * (root + (0.044715 * root) * (x * x)))
+
+
 def iota(shape, dim):
     return lax.broadcasted_iota(jnp.int32, shape, dim)
 
@@ -367,8 +376,9 @@
 
 
 def chem_in_kernel(
-    slots, r_ref, react_ref, w1_ref, h_ref, row_ref, hit_ref, token
+    slots, r_ref, react_ref, w1_ref, h_ref, row_ref, hit_ref, y2_ref, token
 ):
+    store_y_layers(r_ref, y2_ref, place_flags()[7] == 1)
     react = react_ref[...].astype(F32)
     react_b = react.astype(BF16)
     upper = where1(iota((128, 128), 0) <= iota((128, 128), 1))
@@ -401,7 +411,7 @@
     feat = jnp.transpose(feat)[:COMPS].astype(BF16)
     tn = (((0,), (0,)), ((), ()))
     one = lax.dot_general(w1_ref[...], feat, tn, preferred_element_type=F32)
-    h_ref[...] = jax.nn.gelu(one).astype(BF16)
+    h_ref[...] = gelu(one).astype(BF16)
     token[...] = jnp.zeros(token.shape, F32)
 
 
@@ -412,10 +422,11 @@
             jax.ShapeDtypeStruct((layer_one.shape[1], slots), BF16),
             jax.ShapeDtypeStruct((64, slots), BF16),
             jax.ShapeDtypeStruct((slots, 128), BF16),
+            jax.ShapeDtypeStruct((COMPS * 24, 128), BF16),
             token_shape(table),
         ],
         in_specs=[VM] * 3,
-        out_specs=[VM] * 4,
+        out_specs=[VM] * 5,
         compiler_params=GRANT,
         cost_estimate=cost(1),
         name="chem_in",
@@ -424,15 +435,15 @@
 
 def chem_two_kernel(h_ref, w2_ref, out_ref, token):
     half = out_ref.shape[0]
-    out_ref[...] = jax.nn.gelu(dot(w2_ref[pl.ds(0, half), :], h_ref[...])).astype(BF16)
+    out_ref[...] = gelu(dot(w2_ref[pl.ds(0, half), :], h_ref[...])).astype(BF16)
     token[...] = jnp.zeros(token.shape, F32)
 
 
 def chem_three_kernel(h_ref, two_ref, w2_ref, w3_ref, _, out_ref, token):
     half = two_ref.shape[0]
-    rest = jax.nn.gelu(dot(w2_ref[pl.ds(half, half), :], h_ref[...])).astype(BF16)
+    rest = gelu(dot(w2_ref[pl.ds(half, half), :], h_ref[...])).astype(BF16)
     two = jnp.concatenate([two_ref[...], rest], axis=0)
-    out_ref[...] = jax.nn.gelu(dot(w3_ref[...], two)).astype(BF16)
+    out_ref[...] = gelu(dot(w3_ref[...], two)).astype(BF16)
     token[...] = jnp.zeros(token.shape, F32)
 
 
@@ -775,13 +786,13 @@
     panels, react = panel_map.reshape(-1, shape[3]), reacting.reshape(-1, shape[3])
     layers = (layer_one.T, layer_two, layer_three, layer_four)
     packed = pack(flat, panels, react, layers, height)
-    flat, recon, y_first, y_second, table, react, one, four = packed
+    flat, recon, y_first, table, react, one, four = packed
     two, three = layer_two, layer_three
     y_got = [swap(y_first, "gy", 0)]
+    turned, *xs, z_first, z_second, token = turn(recon, pair_x, height)
+    hidden, row_slot, hit, y_second, token_in = chem_in(recon, react, one, slots, table)
     if sizes[1] > 2:
         y_got.append(swap_inner(y_second, "gy", "gz"))
-    turned, *xs, z_first, z_second, token = turn(recon, pair_x, height)
-    hidden, row_slot, hit, token_in = chem_in(recon, react, one, slots, table)
     half, token_two = chem_layer(chem_two_kernel, layer_two.shape[0] // 2, table, hidden, two)
     table = table + token + token_in + token_two
     if ride_y:

time: 22.2 us -> 22.2 us (level)
  no operation moved by 1% of the time
where the time goes in v3:
time: 22.2 us; the launch traced here: 21.9 us
  Pallas kernels  11.1 us (50%)
  starting transfers between devices  9.38 us (42%)
  between operations  0.72 us (3%)
  waiting for transfers between devices  0.54 us (2%)
    ppermute x4, starting transfers between devices, swap(): lax.ppermute(x, axis, [(a, b) for a, b in pairs] + [(b, a) for a, b in pa...  6.96 us
    ppermute x1, starting transfers between devices, body(): rest = lax.ppermute(table, ('gy', 'gz'), pairs)  2.35 us
    pallas_call x2, Pallas kernels, chem_layer(): pl.pallas_call(kernel, out_shape=[jax.ShapeDtypeStruct((rows, operands[0]...  1.68 us
    pallas_call x1, Pallas kernels, flux_z(): pl.pallas_call(lambda *a: flux_z_kernel(len(layers), *a), out_shape=[jax....  1.61 us
    pallas_call x1, Pallas kernels, pack(): pl.pallas_call(pack_kernel, out_shape=outs, in_specs=[HBM] * 5, out_specs...  1.59 us
    pallas_call x1, Pallas kernels, flux_x(): pl.pallas_call(lambda *a: flux_x_kernel(len(layers), *a), out_shape=jax.S...  1.5 us
    pallas_call x1, Pallas kernels, flux_y(): pl.pallas_call(lambda *a: flux_y_kernel(len(layers), *a), out_shape=[jax....  1.31 us
    pallas_call x1, Pallas kernels, chem_in(): pl.pallas_call(lambda *a: chem_in_kernel(slots, *a), out_shape=[jax.Shape...  1.22 us
  transfers between devices with their start and end apart: 6, of which 4 were waited for; matrix products, arithmetic and copies ran while one was open for 0% of the time, Pallas kernels for 41%

profile of v3, /device:TPU:0, one launch (start us, length us, event | category | flops | bytes accessed | tf_op | source)
XLA Modules:
  0.0 21.9 jit_solution(2208352273782480222)
XLA Ops:
  0.6 1.6 %pack.1 = (f32[768,128]{1,0:T(8,128)S(1)}, f32[768,128]{1,0:T(8,128)S(1)}, bf16[304,128]{1,0:T(8,128)(2,1)S(1)}, f32[2,128]{1,0:T(2,128)S(1)}, s32[64,128]{1,0:T...) custom-call(f32[768,128]{1,0:T(8,128)} %bitcast.6, s32[16,128]{1,0:T(8,128)} %bitcast.9, ...), custom_call_target="tpu_custom_call" | custom-call | flops 1600000000 | bytes 5600000 | tf_op jit(solution)/shard_map/pack/pallas_call | solution.py:297
  2.2 3.1 %collective-permute-start = (bf16[304,128]{1,0:T(8,128)(2,1)S(1)}, bf16[304,128]{1,0:T(8,128)(2,1)S(1)}, u32[]{:S(2)}, u32[]{:S(2)}) collective-permute-start(bf16[304,128]{1,0:T(8,128)(2,1)S(1)} %get-tuple-element.37), channel_id=1, source_target_pairs={{0,4},{8,12},{4,0},{12,8},{1,5},{9,13},{5,1},{13,9},{2,6},{10,14},... | collective-permute-start | bytes 233480 | tf_op jit(solution)/shard_map/ppermute | solution.py:743
  5.3 1.2 %chem_in.1 = (bf16[1600,128]{1,0:T(8,128)(2,1)S(1)}, bf16[64,128]{1,0:T(8,128)(2,1)S(1)}, bf16[128,128]{1,0:T(8,128)(2,1)S(1)}, bf16[288,128]{1,0:T(8,128)(2,1)S(1)}, f32[2,128]{1,0:T(2,128)S(1)}) custom-call(f32[768,128]{1,0:T(8,128)S(1)} %get-tuple-element.34.a_0_.r_ref, s32[64,128]{1,0:T(8,128)S(1)} %get-tuple-element.38.a_1_, ...), custom_call_target="tpu_custom_call" | custom-call | flops 800000000 | bytes 2800000 | tf_op jit(solution)/shard_map/chem_in/pallas_call | solution.py:419
  6.6 0.0 copy-start.1
  6.6 0.1 collective-permute-start.1
  6.7 0.3 %turn.1 = (f32[768,128]{1,0:T(8,128)S(1)}, bf16[304,128]{1,0:T(8,128)(2,1)S(1)}, f32[48,128]{1,0:T(8,128)S(1)}, f32[48,128]{1,0:T(8,128)S(1)}, f32[2,128]{1,0:T(2,128)S(1)}) custom-call(f32[768,128]{1,0:T(8,128)S(1)} %get-tuple-element.34.a_0_.r_ref), custom_call_target="tpu_custom_call" | custom-call | flops 800000000 | bytes 2800000 | tf_op jit(solution)/shard_map/turn/pallas_call | solution.py:345
  7.0 0.1 copy-done
  7.1 0.6 %shard_map.86 = (bf16[400,128]{1,0:T(8,128)(2,1)S(1)}, f32[2,128]{1,0:T(2,128)S(1)}) custom-call(bf16[1600,128]{1,0:T(8,128)(2,1)S(1)} %get-tuple-element.46.h_ref, bf16[800,1600]{1,0:T(8,128)(2,1)S(1)} %copy-done), custom_call_target="tpu_custom_call" | custom-call | flops 800000000 | bytes 2800000 | tf_op jit(solution)/shard_map/pallas_call | solution.py:451
  7.7 0.1 collective-permute-done.a_1_
  7.7 0.4 %collective-permute-start.2 = (f32[48,128]{1,0:T(8,128)S(1)}, f32[48,128]{1,0:T(8,128)S(1)}, u32[]{:S(2)}, u32[]{:S(2)}) collective-permute-start(f32[48,128]{1,0:T(8,128)S(1)} %get-tuple-element.66), channel_id=1, source_target_pairs={{0,1},{2,3},{1,0},{3,2},{4,5},{6,7},{5,4},{7,6},{8,9},{10,11},{9,8... | collective-permute-start | bytes 73736 | tf_op jit(solution)/shard_map/ppermute | solution.py:743
  8.2 1.1 %shard_map.87 = (bf16[400,128]{1,0:T(8,128)(2,1)S(1)}, f32[2,128]{1,0:T(2,128)S(1)}) custom-call(bf16[1600,128]{1,0:T(8,128)(2,1)S(1)} %get-tuple-element.46.h_ref, bf16[400,128]{1,0:T(8,128)(2,1)S(1)} %get-tuple-element.49.two_ref, bf16[800,1600]{1,0:T(8,128)(2,1)S(1)} %copy-done, bf16[400,800]{1,0:T(8,128)(2,1)S(1)} %copy-done.1, ...), custom_call_target="tpu_custom_call" | custom-call | flops 800000000 | bytes 2800000 | tf_op jit(solution)/shard_map/pallas_call | solution.py:451
  9.3 1.8 %collective-permute-start.3 = (f32[48,128]{1,0:T(8,128)S(1)}, f32[48,128]{1,0:T(8,128)S(1)}, u32[]{:S(2)}, u32[]{:S(2)}) collective-permute-start(f32[48,128]{1,0:T(8,128)S(1)} %constant_dynamic-update-slice_fusion), channel_id=1, source_target_pairs={{1,2},{0,3},{2,1},{3,0},{5,6},{4,7},{6,5},{7,4},{9,10},{8,11},{10,... | collective-permute-start | bytes 73736 | tf_op jit(solution)/shard_map/ppermute | solution.py:743
  11.1 0.0 collective-permute-done.1.a_2_
  11.1 1.3 %flux_y.1 = (f32[768,128]{1,0:T(8,128)S(1)}, f32[2,128]{1,0:T(2,128)S(1)}) custom-call(f32[768,128]{1,0:T(8,128)S(1)} %get-tuple-element.34.a_0_.r_ref, bf16[304,128]{1,0:T(8,128)(2,1)S(1)} %collective-permute-done.a_1_, bf16[288,128]{1,0:T(8,128)(2,1)S(1)} %collective-permute-done.1.a_2_), custom_call_target="tpu_custom_call" | custom-call | flops 1600000000 | bytes 5600000 | tf_op jit(solution)/shard_map/flux_y/pallas_call | solution.py:711
  12.4 0.2 %collective-permute-done.3.a_3_ = f32[48,128]{1,0:T(8,128)S(1)} collective-permute-done((f32[48,128]{1,0:T(8,128)S(1)}, f32[48,128]{1,0:T(8,128)S(1)}, u32[]{:S(2)}, u32[]{:S(2)}) %collective-permute-start.3) | collective-permute-done | bytes 24608 | tf_op jit(solution)/shard_map/ppermute | solution.py:743
  12.7 1.6 %collective-permute-start.4 = (bf16[304,128]{1,0:T(8,128)(2,1)S(1)}, bf16[304,128]{1,0:T(8,128)(2,1)S(1)}, u32[]{:S(2)}, u32[]{:S(2)}) collective-permute-start(bf16[304,128]{1,0:T(8,128)(2,1)S(1)} %put_table.1), channel_id=1, source_target_pairs={{0,16},{16,0},{1,17},{17,1},{2,18},{18,2},{3,19},{19,3},{4,20},{20... | collective-permute-start | bytes 233480 | tf_op jit(solution)/shard_map/ppermute | solution.py:743
  14.3 1.6 %flux_z.1 = (f32[768,128]{1,0:T(8,128)S(1)}, f32[2,128]{1,0:T(2,128)S(1)}) custom-call(f32[768,128]{1,0:T(8,128)S(1)} %get-tuple-element.36.a_0_, f32[768,128]{1,0:T(8,128)S(1)} %get-tuple-element.41.a_1_, f32[48,128]{1,0:T(8,128)S(1)} %collective-permute-done.2.a_2_, f32[48,128]{1,0:T(8,128)S(1)} %collective-permute-done.3.a_3_), custom_call_target="tpu_custom_call" | custom-call | flops 1600000000 | bytes 5600000 | tf_op jit(solution)/shard_map/flux_z/pallas_call | solution.py:724
  15.9 0.7 %chem_out.1 = (f32[768,128]{1,0:T(8,128)S(1)}, f32[2,128]{1,0:T(2,128)S(1)}) custom-call(bf16[400,128]{1,0:T(8,128)(2,1)S(1)} %get-tuple-element.52.h_ref, bf16[12,400]{1,0:T(8,128)(2,1)S(1)} %get-tuple-element.53.w4_ref, bf16[64,128]{1,0:T(8,128)(2,1)S(1)} %get-tuple-element.54.row_ref, bf16[128,128]{1,0:T(8,128)(2,1)S(1)} %get-tuple-element.55.hit_ref, ...), custom_call_target="tpu_custom_call" | custom-call | flops 800000000 | bytes 2800000 | tf_op jit(solution)/shard_map/chem_out/pallas_call | solution.py:477
  16.6 0.6 %flux_x_inner.1 = (f32[864,128]{1,0:T(8,128)S(1)}, f32[864,128]{1,0:T(8,128)S(1)}, f32[192,128]{1,0:T(8,128)S(1)}, f32[12,64,128]{2,1,0:T(8,128)S(1)}, f32[2,128]{1,0:T(2,128)S(1)}) custom-call(f32[768,128]{1,0:T(8,128)S(1)} %get-tuple-element.35.f_ref, f32[768,128]{1,0:T(8,128)S(1)} %get-tuple-element.34.a_0_.r_ref, ...), custom_call_target="tpu_custom_call" | custom-call | flops 800000000 | bytes 2800000 | tf_op jit(solution)/shard_map/flux_x_inner/pallas_call | solution.py:678
  17.2 0.1 collective-permute-done.4.a_5_
  17.3 2.3 %collective-permute-start.5 = (f32[2,128]{1,0:T(2,128)S(1)}, f32[2,128]{1,0:T(2,128)S(1)}, u32[]{:S(2)}, u32[]{:S(2)}) collective-permute-start(f32[2,128]{1,0:T(2,128)S(1)} %add_add_fusion.a_0_), channel_id=1, source_target_pairs={{0,9},{1,8},{2,11},{3,10},{4,13},{5,12},{6,15},{7,14},{8,1},{9,0},... | collective-permute-start | bytes 3080 | tf_op jit(solution)/shard_map/ppermute | solution.py:834
  19.7 1.5 %flux_x.1 = f32[12,64,128]{2,1,0:T(8,128)} custom-call(f32[768,128]{1,0:T(8,128)S(1)} %get-tuple-element.34.a_0_.r_ref, f32[864,128]{1,0:T(8,128)S(1)} %get-tuple-element.58.a_1_, f32[864,128]{1,0:T(8,128)S(1)} %get-tuple-element.59.a_2_, f32[192,128]{1,0:T(8,128)S(1)} %get-tuple-element.60.a_3_, f32[12,64,128]{2,1,0:T(8,128)S(1)} %get-tuple-element.61.a_4_, ...), custom_call_target="tpu_custom_call" | custom-call | flops 1600000000 | bytes 5600000 | tf_op jit(solution)/shard_map/flux_x/pallas_call | solution.py:696
  21.2 0.1 collective-permute-done.5.a_1_
  21.3 0.6 %impulse.1 = f32[1,8]{1,0:T(1,128)} custom-call(f32[2,128]{1,0:T(2,128)S(1)} %add_add_fusion.a_0_, f32[2,128]{1,0:T(2,128)S(1)} %collective-permute-done.5.a_1_), custom_call_target="tpu_custom_call" | custom-call | flops 400000000 | bytes 1400000 | tf_op jit(solution)/shard_map/impulse/pallas_call | solution.py:653
  (10 shorter events, 0.1 us)
Async XLA Ops:
  2.2 5.5 %collective-permute-start = (bf16[304,128]{1,0:T(8,128)(2,1)S(1)}, bf16[304,128]{1,0:T(8,128)(2,1)S(1)}, u32[]{:S(2)}, u32[]{:S(2)}) collective-permute-start(bf16[304,128]{1,0:T(8,128)(2,1)S(1)} %get-tuple-element.37), channel_id=1, source_target_pairs={{0,4},{8,12},{4,0},{12,8},{1,5},{9,13},{5,1},{13,9},{2,6},{10,14},... | collective-permute-start | bytes 233480 | tf_op jit(solution)/shard_map/ppermute | solution.py:743
  5.3 1.8 %copy-start = (bf16[800,1600]{1,0:T(8,128)(2,1)S(1)}, bf16[800,1600]{1,0:T(8,128)(2,1)}, u32[]{:S(2)}) copy-start(bf16[800,1600]{1,0:T(8,128)(2,1)} %w2_ref.3) | copy-start | bytes 7680004
  6.6 1.6 %copy-start.1 = (bf16[400,800]{1,0:T(8,128)(2,1)S(1)}, bf16[400,800]{1,0:T(8,128)(2,1)}, u32[]{:S(2)}) copy-start(bf16[400,800]{1,0:T(8,128)(2,1)} %w3_ref.1) | copy-start | bytes 1920004
  6.6 4.5 %collective-permute-start.1 = (bf16[288,128]{1,0:T(8,128)(2,1)S(1)}, bf16[288,128]{1,0:T(8,128)(2,1)S(1)}, u32[]{:S(2)}, u32[]{:S(2)}) collective-permute-start(bf16[288,128]{1,0:T(8,128)(2,1)S(1)} %get-tuple-element.40), channel_id=1, source_target_pairs={{0,1},{1,0},{2,3},{3,2},{4,8},{5,9},{6,10},{7,11},{8,4},{9,5},{10,... | collective-permute-start | bytes 221192 | tf_op jit(solution)/shard_map/ppermute | solution.py:756
  7.7 1.6 %collective-permute-start.2 = (f32[48,128]{1,0:T(8,128)S(1)}, f32[48,128]{1,0:T(8,128)S(1)}, u32[]{:S(2)}, u32[]{:S(2)}) collective-permute-start(f32[48,128]{1,0:T(8,128)S(1)} %get-tuple-element.66), channel_id=1, source_target_pairs={{0,1},{2,3},{1,0},{3,2},{4,5},{6,7},{5,4},{7,6},{8,9},{10,11},{9,8... | collective-permute-start | bytes 73736 | tf_op jit(solution)/shard_map/ppermute | solution.py:743
  9.3 3.3 %collective-permute-start.3 = (f32[48,128]{1,0:T(8,128)S(1)}, f32[48,128]{1,0:T(8,128)S(1)}, u32[]{:S(2)}, u32[]{:S(2)}) collective-permute-start(f32[48,128]{1,0:T(8,128)S(1)} %constant_dynamic-update-slice_fusion), channel_id=1, source_target_pairs={{1,2},{0,3},{2,1},{3,0},{5,6},{4,7},{6,5},{7,4},{9,10},{8,11},{10,... | collective-permute-start | bytes 73736 | tf_op jit(solution)/shard_map/ppermute | solution.py:743
  12.7 4.7 %collective-permute-start.4 = (bf16[304,128]{1,0:T(8,128)(2,1)S(1)}, bf16[304,128]{1,0:T(8,128)(2,1)S(1)}, u32[]{:S(2)}, u32[]{:S(2)}) collective-permute-start(bf16[304,128]{1,0:T(8,128)(2,1)S(1)} %put_table.1), channel_id=1, source_target_pairs={{0,16},{16,0},{1,17},{17,1},{2,18},{18,2},{3,19},{19,3},{4,20},{20... | collective-permute-start | bytes 233480 | tf_op jit(solution)/shard_map/ppermute | solution.py:743
  17.3 4.0 %collective-permute-start.5 = (f32[2,128]{1,0:T(2,128)S(1)}, f32[2,128]{1,0:T(2,128)S(1)}, u32[]{:S(2)}, u32[]{:S(2)}) collective-permute-start(f32[2,128]{1,0:T(2,128)S(1)} %add_add_fusion.a_0_), channel_id=1, source_target_pairs={{0,9},{1,8},{2,11},{3,10},{4,13},{5,12},{6,15},{7,14},{8,1},{9,0},... | collective-permute-start | bytes 3080 | tf_op jit(solution)/shard_map/ppermute | solution.py:834

commit v4 on v3

--- a/solution.py
+++ b/solution.py
@@ -168,11 +168,11 @@
 
 
 def pack_kernel(*refs):
-    f_hbm, map_hbm, *sources = refs[:5]
-    f_ref, r_ref, y1_ref, table_ref, *kept = refs[5:12]
-    buf, map_ref, sems = refs[12:]
+    f_hbm, map_hbm, *sources = refs[:3]
+    f_ref, r_ref, y1_ref, table_ref, *kept = refs[3:8]
+    buf, map_ref, sems = refs[8:]
     pairs = [(f_hbm, f_ref, 8), (map_hbm, map_ref, 1)]
-    pairs += list(zip(sources, kept, (1, 1, 1)))
+    pairs += list(zip(sources, kept, (1,)))
     waits = [fetch(a, b, sems.at[i], parts) for i, (a, b, parts) in enumerate(pairs)]
     flags = place_flags()
     waits[0]()
@@ -291,23 +291,23 @@
     outs = [whole, whole]
     outs.append(jax.ShapeDtypeStruct((COMPS * 24 + load_rows(height), 128), BF16))
     outs.append(jax.ShapeDtypeStruct((height, 128), F32))
-    one, _, _, four = layers
-    kept = [jax.ShapeDtypeStruct(x.shape, x.dtype) for x in (react, one, four)]
+    one, two, three, four = layers
+    kept = [jax.ShapeDtypeStruct(x.shape, x.dtype) for x in (react,)]
     outs += kept
     return pl.pallas_call(
         pack_kernel,
         out_shape=outs,
-        in_specs=[HBM] * 5,
+        in_specs=[HBM] * 3,
         out_specs=[VM] * len(outs),
         scratch_shapes=[
             pltpu.VMEM((128, 128), F32),
             pltpu.VMEM(panels.shape, jnp.int32),
-            pltpu.SemaphoreType.DMA((5,)),
+            pltpu.SemaphoreType.DMA((3,)),
         ],
         compiler_params=GRANT,
         cost_estimate=cost(2),
         name="pack",
-    )(*map(in_hbm, (fields, panels, react, one, four)))
+    )(*map(in_hbm, (fields, panels, react)))
 
 
 def turn_kernel(pair_x, r_ref, zt_ref, *refs):
@@ -786,8 +786,9 @@
     panels, react = panel_map.reshape(-1, shape[3]), reacting.reshape(-1, shape[3])
     layers = (layer_one.T, layer_two, layer_three, layer_four)
     packed = pack(flat, panels, react, layers, height)
-    flat, recon, y_first, table, react, one, four = packed
-    two, three = layer_two, layer_three
+    flat, recon, y_first, table, react = packed
+    one = layers[0]
+    two, three, four = layer_two, layer_three, layer_four
     y_got = [swap(y_first, "gy", 0)]
     turned, *xs, z_first, z_second, token = turn(recon, pair_x, height)
     hidden, row_slot, hit, y_second, token_in = chem_in(recon, react, one, slots, table)

time: 22.2 us -> 22.2 us (level)
  no operation moved by 1% of the time
where the time goes in v4:
time: 22.2 us; the launch traced here: 21.9 us
  Pallas kernels  11.1 us (50%)
  starting transfers between devices  9.4 us (42%)
  between operations  0.74 us (3%)
  waiting for transfers between devices  0.5 us (2%)
    ppermute x4, starting transfers between devices, swap(): lax.ppermute(x, axis, [(a, b) for a, b in pairs] + [(b, a) for a, b in pa...  6.96 us
    ppermute x1, starting transfers between devices, body(): rest = lax.ppermute(table, ('gy', 'gz'), pairs)  2.37 us
    pallas_call x2, Pallas kernels, chem_layer(): pl.pallas_call(kernel, out_shape=[jax.ShapeDtypeStruct((rows, operands[0]...  1.68 us
    pallas_call x1, Pallas kernels, flux_z(): pl.pallas_call(lambda *a: flux_z_kernel(len(layers), *a), out_shape=[jax....  1.61 us
    pallas_call x1, Pallas kernels, pack(): pl.pallas_call(pack_kernel, out_shape=outs, in_specs=[HBM] * 3, out_specs...  1.58 us
    pallas_call x1, Pallas kernels, flux_x(): pl.pallas_call(lambda *a: flux_x_kernel(len(layers), *a), out_shape=jax.S...  1.5 us
    pallas_call x1, Pallas kernels, flux_y(): pl.pallas_call(lambda *a: flux_y_kernel(len(layers), *a), out_shape=[jax....  1.31 us
    pallas_call x1, Pallas kernels, chem_in(): pl.pallas_call(lambda *a: chem_in_kernel(slots, *a), out_shape=[jax.Shape...  1.22 us
  transfers between devices with their start and end apart: 6, of which 4 were waited for; matrix products, arithmetic and copies ran while one was open for 0% of the time, Pallas kernels for 41%

profile of v4, /device:TPU:0, one launch (start us, length us, event | category | flops | bytes accessed | tf_op | source)
XLA Modules:
  0.0 21.9 jit_solution(118678128844304108)
XLA Ops:
  0.6 1.6 %pack.1 = (f32[768,128]{1,0:T(8,128)S(1)}, f32[768,128]{1,0:T(8,128)S(1)}, bf16[304,128]{1,0:T(8,128)(2,1)S(1)}, f32[2,128]{1,0:T(2,128)S(1)}, s32[64,128]{1,0:T(8,128)S(1)}) custom-call(f32[768,128]{1,0:T(8,128)} %bitcast.7, s32[16,128]{1,0:T(8,128)} %bitcast.9, s32[64,128]{1,0:T(8,128)} %bitcast.8), custom_call_target="tpu_custom_call" | custom-call | flops 1600000000 | bytes 5600000 | tf_op jit(solution)/shard_map/pack/pallas_call | solution.py:297
  2.2 3.1 %collective-permute-start = (bf16[304,128]{1,0:T(8,128)(2,1)S(1)}, bf16[304,128]{1,0:T(8,128)(2,1)S(1)}, u32[]{:S(2)}, u32[]{:S(2)}) collective-permute-start(bf16[304,128]{1,0:T(8,128)(2,1)S(1)} %get-tuple-element.35), channel_id=1, source_target_pairs={{0,4},{8,12},{4,0},{12,8},{1,5},{9,13},{5,1},{13,9},{2,6},{10,14},... | collective-permute-start | bytes 233480 | tf_op jit(solution)/shard_map/ppermute | solution.py:743
  5.4 1.2 %chem_in.1 = (bf16[1600,128]{1,0:T(8,128)(2,1)S(1)}, bf16[64,128]{1,0:T(8,128)(2,1)S(1)}, bf16[128,128]{1,0:T(8,128)(2,1)S(1)}, bf16[288,128]{1,0:T(8,128)(2,1)S(1)}, f32[2,128]{1,0:T(2,128)S(1)}) custom-call(f32[768,128]{1,0:T(8,128)S(1)} %get-tuple-element.32.a_0_.r_ref, s32[64,128]{1,0:T(8,128)S(1)} %get-tuple-element.36.a_1_, bf16[12,1600]{1,0:T(8,128)(2,1)S(1)} %bitcast.6), custom_call_target="tpu_custom_call" | custom-call | flops 800000000 | bytes 2800000 | tf_op jit(solution)/shard_map/chem_in/pallas_call | solution.py:419
  6.6 0.0 copy-start.1
  6.6 0.1 collective-permute-start.1
  6.7 0.3 %turn.1 = (f32[768,128]{1,0:T(8,128)S(1)}, bf16[304,128]{1,0:T(8,128)(2,1)S(1)}, f32[48,128]{1,0:T(8,128)S(1)}, f32[48,128]{1,0:T(8,128)S(1)}, f32[2,128]{1,0:T(2,128)S(1)}) custom-call(f32[768,128]{1,0:T(8,128)S(1)} %get-tuple-element.32.a_0_.r_ref), custom_call_target="tpu_custom_call" | custom-call | flops 800000000 | bytes 2800000 | tf_op jit(solution)/shard_map/turn/pallas_call | solution.py:345
  7.0 0.1 copy-done
  7.1 0.6 %shard_map.86 = (bf16[400,128]{1,0:T(8,128)(2,1)S(1)}, f32[2,128]{1,0:T(2,128)S(1)}) custom-call(bf16[1600,128]{1,0:T(8,128)(2,1)S(1)} %get-tuple-element.43.h_ref, bf16[800,1600]{1,0:T(8,128)(2,1)S(1)} %copy-done), custom_call_target="tpu_custom_call" | custom-call | flops 800000000 | bytes 2800000 | tf_op jit(solution)/shard_map/pallas_call | solution.py:451
  7.7 0.1 collective-permute-done.a_1_
  7.7 0.4 %collective-permute-start.2 = (f32[48,128]{1,0:T(8,128)S(1)}, f32[48,128]{1,0:T(8,128)S(1)}, u32[]{:S(2)}, u32[]{:S(2)}) collective-permute-start(f32[48,128]{1,0:T(8,128)S(1)} %get-tuple-element.62), channel_id=1, source_target_pairs={{0,1},{2,3},{1,0},{3,2},{4,5},{6,7},{5,4},{7,6},{8,9},{10,11},{9,8... | collective-permute-start | bytes 73736 | tf_op jit(solution)/shard_map/ppermute | solution.py:743
  8.2 1.1 %shard_map.87 = (bf16[400,128]{1,0:T(8,128)(2,1)S(1)}, f32[2,128]{1,0:T(2,128)S(1)}) custom-call(bf16[1600,128]{1,0:T(8,128)(2,1)S(1)} %get-tuple-element.43.h_ref, bf16[400,128]{1,0:T(8,128)(2,1)S(1)} %get-tuple-element.46.two_ref, bf16[800,1600]{1,0:T(8,128)(2,1)S(1)} %copy-done, bf16[400,800]{1,0:T(8,128)(2,1)S(1)} %copy-done.1, ...), custom_call_target="tpu_custom_call" | custom-call | flops 800000000 | bytes 2800000 | tf_op jit(solution)/shard_map/pallas_call | solution.py:451
  9.3 1.8 %collective-permute-start.3 = (f32[48,128]{1,0:T(8,128)S(1)}, f32[48,128]{1,0:T(8,128)S(1)}, u32[]{:S(2)}, u32[]{:S(2)}) collective-permute-start(f32[48,128]{1,0:T(8,128)S(1)} %constant_dynamic-update-slice_fusion), channel_id=1, source_target_pairs={{1,2},{0,3},{2,1},{3,0},{5,6},{4,7},{6,5},{7,4},{9,10},{8,11},{10,... | collective-permute-start | bytes 73736 | tf_op jit(solution)/shard_map/ppermute | solution.py:743
  11.1 0.0 collective-permute-done.1.a_2_
  11.1 1.3 %flux_y.1 = (f32[768,128]{1,0:T(8,128)S(1)}, f32[2,128]{1,0:T(2,128)S(1)}) custom-call(f32[768,128]{1,0:T(8,128)S(1)} %get-tuple-element.32.a_0_.r_ref, bf16[304,128]{1,0:T(8,128)(2,1)S(1)} %collective-permute-done.a_1_, bf16[288,128]{1,0:T(8,128)(2,1)S(1)} %collective-permute-done.1.a_2_), custom_call_target="tpu_custom_call" | custom-call | flops 1600000000 | bytes 5600000 | tf_op jit(solution)/shard_map/flux_y/pallas_call | solution.py:711
  12.4 0.2 %collective-permute-done.3.a_3_ = f32[48,128]{1,0:T(8,128)S(1)} collective-permute-done((f32[48,128]{1,0:T(8,128)S(1)}, f32[48,128]{1,0:T(8,128)S(1)}, u32[]{:S(2)}, u32[]{:S(2)}) %collective-permute-start.3) | collective-permute-done | bytes 24608 | tf_op jit(solution)/shard_map/ppermute | solution.py:743
  12.7 1.6 %collective-permute-start.4 = (bf16[304,128]{1,0:T(8,128)(2,1)S(1)}, bf16[304,128]{1,0:T(8,128)(2,1)S(1)}, u32[]{:S(2)}, u32[]{:S(2)}) collective-permute-start(bf16[304,128]{1,0:T(8,128)(2,1)S(1)} %put_table.1), channel_id=1, source_target_pairs={{0,16},{16,0},{1,17},{17,1},{2,18},{18,2},{3,19},{19,3},{4,20},{20... | collective-permute-start | bytes 233480 | tf_op jit(solution)/shard_map/ppermute | solution.py:743
  14.3 1.6 %flux_z.1 = (f32[768,128]{1,0:T(8,128)S(1)}, f32[2,128]{1,0:T(2,128)S(1)}) custom-call(f32[768,128]{1,0:T(8,128)S(1)} %get-tuple-element.34.a_0_, f32[768,128]{1,0:T(8,128)S(1)} %get-tuple-element.38.a_1_, f32[48,128]{1,0:T(8,128)S(1)} %collective-permute-done.2.a_2_, f32[48,128]{1,0:T(8,128)S(1)} %collective-permute-done.3.a_3_), custom_call_target="tpu_custom_call" | custom-call | flops 1600000000 | bytes 5600000 | tf_op jit(solution)/shard_map/flux_z/pallas_call | solution.py:724
  15.9 0.7 %chem_out.1 = (f32[768,128]{1,0:T(8,128)S(1)}, f32[2,128]{1,0:T(2,128)S(1)}) custom-call(bf16[400,128]{1,0:T(8,128)(2,1)S(1)} %get-tuple-element.49.h_ref, bf16[12,400]{1,0:T(8,128)(2,1)S(1)} %copy-done.3, bf16[64,128]{1,0:T(8,128)(2,1)S(1)} %get-tuple-element.50.row_ref, bf16[128,128]{1,0:T(8,128)(2,1)S(1)} %get-tuple-element.51.hit_ref, ...), custom_call_target="tpu_custom_call" | custom-call | flops 800000000 | bytes 2800000 | tf_op jit(solution)/shard_map/chem_out/pallas_call | solution.py:477
  16.6 0.6 %flux_x_inner.1 = (f32[864,128]{1,0:T(8,128)S(1)}, f32[864,128]{1,0:T(8,128)S(1)}, f32[192,128]{1,0:T(8,128)S(1)}, f32[12,64,128]{2,1,0:T(8,128)S(1)}, f32[2,128]{1,0:T(2,128)S(1)}) custom-call(f32[768,128]{1,0:T(8,128)S(1)} %get-tuple-element.33.f_ref, f32[768,128]{1,0:T(8,128)S(1)} %get-tuple-element.32.a_0_.r_ref, ...), custom_call_target="tpu_custom_call" | custom-call | flops 800000000 | bytes 2800000 | tf_op jit(solution)/shard_map/flux_x_inner/pallas_call | solution.py:678
  17.2 0.1 collective-permute-done.4.a_5_
  17.3 2.4 %collective-permute-start.5 = (f32[2,128]{1,0:T(2,128)S(1)}, f32[2,128]{1,0:T(2,128)S(1)}, u32[]{:S(2)}, u32[]{:S(2)}) collective-permute-start(f32[2,128]{1,0:T(2,128)S(1)} %add_add_fusion.a_0_), channel_id=1, source_target_pairs={{0,9},{1,8},{2,11},{3,10},{4,13},{5,12},{6,15},{7,14},{8,1},{9,0},... | collective-permute-start | bytes 3080 | tf_op jit(solution)/shard_map/ppermute | solution.py:835
  19.7 1.5 %flux_x.1 = f32[12,64,128]{2,1,0:T(8,128)} custom-call(f32[768,128]{1,0:T(8,128)S(1)} %get-tuple-element.32.a_0_.r_ref, f32[864,128]{1,0:T(8,128)S(1)} %get-tuple-element.54.a_1_, f32[864,128]{1,0:T(8,128)S(1)} %get-tuple-element.55.a_2_, f32[192,128]{1,0:T(8,128)S(1)} %get-tuple-element.56.a_3_, f32[12,64,128]{2,1,0:T(8,128)S(1)} %get-tuple-element.57.a_4_, ...), custom_call_target="tpu_custom_call" | custom-call | flops 1600000000 | bytes 5600000 | tf_op jit(solution)/shard_map/flux_x/pallas_call | solution.py:696
  21.2 0.1 collective-permute-done.5.a_1_
  21.3 0.6 %impulse.1 = f32[1,8]{1,0:T(1,128)} custom-call(f32[2,128]{1,0:T(2,128)S(1)} %add_add_fusion.a_0_, f32[2,128]{1,0:T(2,128)S(1)} %collective-permute-done.5.a_1_), custom_call_target="tpu_custom_call" | custom-call | flops 400000000 | bytes 1400000 | tf_op jit(solution)/shard_map/impulse/pallas_call | solution.py:653
  (14 shorter events, 0.1 us)
Async XLA Ops:
  0.6 4.7 %copy-start.2 = (bf16[1600,12]{0,1:T(8,128)(2,1)S(1)}, bf16[1600,12]{0,1:T(8,128)(2,1)}, u32[]{:S(2)}) copy-start(bf16[1600,12]{0,1:T(8,128)(2,1)} %param.10) | copy-start | bytes 115204
  2.2 5.5 %collective-permute-start = (bf16[304,128]{1,0:T(8,128)(2,1)S(1)}, bf16[304,128]{1,0:T(8,128)(2,1)S(1)}, u32[]{:S(2)}, u32[]{:S(2)}) collective-permute-start(bf16[304,128]{1,0:T(8,128)(2,1)S(1)} %get-tuple-element.35), channel_id=1, source_target_pairs={{0,4},{8,12},{4,0},{12,8},{1,5},{9,13},{5,1},{13,9},{2,6},{10,14},... | collective-permute-start | bytes 233480 | tf_op jit(solution)/shard_map/ppermute | solution.py:743
  5.3 1.8 %copy-start = (bf16[800,1600]{1,0:T(8,128)(2,1)S(1)}, bf16[800,1600]{1,0:T(8,128)(2,1)}, u32[]{:S(2)}) copy-start(bf16[800,1600]{1,0:T(8,128)(2,1)} %w2_ref.3) | copy-start | bytes 7680004
  6.6 1.6 %copy-start.1 = (bf16[400,800]{1,0:T(8,128)(2,1)S(1)}, bf16[400,800]{1,0:T(8,128)(2,1)}, u32[]{:S(2)}) copy-start(bf16[400,800]{1,0:T(8,128)(2,1)} %w3_ref.1) | copy-start | bytes 1920004
  6.6 4.5 %collective-permute-start.1 = (bf16[288,128]{1,0:T(8,128)(2,1)S(1)}, bf16[288,128]{1,0:T(8,128)(2,1)S(1)}, u32[]{:S(2)}, u32[]{:S(2)}) collective-permute-start(bf16[288,128]{1,0:T(8,128)(2,1)S(1)} %get-tuple-element.37), channel_id=1, source_target_pairs={{0,1},{1,0},{2,3},{3,2},{4,8},{5,9},{6,10},{7,11},{8,4},{9,5},{10,... | collective-permute-start | bytes 221192 | tf_op jit(solution)/shard_map/ppermute | solution.py:756
  7.7 1.6 %collective-permute-start.2 = (f32[48,128]{1,0:T(8,128)S(1)}, f32[48,128]{1,0:T(8,128)S(1)}, u32[]{:S(2)}, u32[]{:S(2)}) collective-permute-start(f32[48,128]{1,0:T(8,128)S(1)} %get-tuple-element.62), channel_id=1, source_target_pairs={{0,1},{2,3},{1,0},{3,2},{4,5},{6,7},{5,4},{7,6},{8,9},{10,11},{9,8... | collective-permute-start | bytes 73736 | tf_op jit(solution)/shard_map/ppermute | solution.py:743
  9.3 3.3 %collective-permute-start.3 = (f32[48,128]{1,0:T(8,128)S(1)}, f32[48,128]{1,0:T(8,128)S(1)}, u32[]{:S(2)}, u32[]{:S(2)}) collective-permute-start(f32[48,128]{1,0:T(8,128)S(1)} %constant_dynamic-update-slice_fusion), channel_id=1, source_target_pairs={{1,2},{0,3},{2,1},{3,0},{5,6},{4,7},{6,5},{7,4},{9,10},{8,11},{10,... | collective-permute-start | bytes 73736 | tf_op jit(solution)/shard_map/ppermute | solution.py:743
  12.7 4.6 %collective-permute-start.4 = (bf16[304,128]{1,0:T(8,128)(2,1)S(1)}, bf16[304,128]{1,0:T(8,128)(2,1)S(1)}, u32[]{:S(2)}, u32[]{:S(2)}) collective-permute-start(bf16[304,128]{1,0:T(8,128)(2,1)S(1)} %put_table.1), channel_id=1, source_target_pairs={{0,16},{16,0},{1,17},{17,1},{2,18},{18,2},{3,19},{19,3},{4,20},{20... | collective-permute-start | bytes 233480 | tf_op jit(solution)/shard_map/ppermute | solution.py:743
  14.3 1.6 %copy-start.3 = (bf16[12,400]{1,0:T(8,128)(2,1)S(1)}, bf16[12,400]{1,0:T(8,128)(2,1)}, u32[]{:S(2)}) copy-start(bf16[12,400]{1,0:T(8,128)(2,1)} %w4_ref.1) | copy-start | bytes 28804
  17.3 4.0 %collective-permute-start.5 = (f32[2,128]{1,0:T(2,128)S(1)}, f32[2,128]{1,0:T(2,128)S(1)}, u32[]{:S(2)}, u32[]{:S(2)}) collective-permute-start(f32[2,128]{1,0:T(2,128)S(1)} %add_add_fusion.a_0_), channel_id=1, source_target_pairs={{0,9},{1,8},{2,11},{3,10},{4,13},{5,12},{6,15},{7,14},{8,1},{9,0},... | collective-permute-start | bytes 3080 | tf_op jit(solution)/shard_map/ppermute | solution.py:835
